TPU v7x, 256 devices: a whole 4x4x8 slice. The times are simulated.
256 devices in a mesh: expert: 128 (over z, y, x), dp: 2 (over core).
Axes of the slice: x: 4, y: 4, z: 8, core: 2. Of those that a mesh axis runs over, the one named last changes fastest.
Arguments:
- hidden_in: float32 [12288, 2048], P(('expert', 'dp')), may hold values from -6 to 6
- out_grad: float32 [12288, 2048], P(('expert', 'dp')), may hold values from -6 to 6
- route_prob: float32 [12288, 8], P(('expert', 'dp')), may hold values from 0.03 to 0.6
- route_ids: int32 [12288, 8], P(('expert', 'dp')), may hold values from 0 to 127, all different within a row; in each aligned block of 48 rows (0 to 47, 48 to 95, ...) at most 4 rows name the same one
- w_gate: bfloat16 [128, 2048, 768], P('expert', None, 'dp'), may hold values from -0.125 to 0.125
- w_up: bfloat16 [128, 2048, 768], P('expert', None, 'dp'), may hold values from -0.125 to 0.125
- w_down: bfloat16 [128, 2048, 768], P('expert', None, 'dp'), may hold values from -0.21875 to 0.21875
Outputs:
- input_grad: float32 [12288, 2048], P(('expert', 'dp'))
- grad_gate: bfloat16 [128, 2048, 768], P('expert', None, 'dp')
- grad_up: bfloat16 [128, 2048, 768], P('expert', None, 'dp')
- grad_down: bfloat16 [128, 2048, 768], P('expert', None, 'dp')
Inputs may be any that keep to these rules, and one draw needn't show every extreme that they name: `route_ids`: each row names 8 different experts. Among the 48 tokens of one device no expert is named more than 4 times; in every draw some expert is named exactly 4 times by the tokens of some device.
All inputs are finite; a program needn't handle non-finite values.
Results may differ from a plain program's by a relative error of at most 0.0089.
Values may be sent and summed in bfloat16 or wider, within the bound.
No kernel may reach another device: no remote copies, remote signals or barrier semaphores. Data moves between devices by JAX's collectives and lax.ppermute only.
A program may use at most 128 MiB of HBM per device.

v0:
```python
import jax
import jax.numpy as jnp
from jax import lax
from jax.experimental import pallas as pl
from jax.experimental.pallas import tpu as pltpu
from jax.sharding import Mesh, PartitionSpec as P

F32 = jnp.float32
BF16 = jnp.bfloat16
PLANE = 16
LANES = 128
SCOPED = 8 << 20
IN_HBM = pl.BlockSpec(memory_space=pltpu.HBM)
IN_VMEM = pl.BlockSpec(memory_space=pltpu.VMEM)


def mm(a, b, dims):
    return lax.dot_general(a, b, ((dims[0], dims[1]), ((), ())), preferred_element_type=F32)


def before(count, block):
    i = lax.broadcasted_iota(jnp.int32, (count, count), 0)
    j = lax.broadcasted_iota(jnp.int32, (count, count), 1)
    return ((i < j) & (i // block == j // block)).astype(BF16)


def named_by(expert, ids_t, prob_t):
    named = jnp.zeros(jnp.broadcast_shapes(expert.shape, (1, ids_t.shape[1])), F32)
    prob = named
    for k in range(ids_t.shape[0]):
        hit = expert == ids_t[k][None, :]
        named = jnp.where(hit, 1.0, named)
        if prob_t is not None:
            prob = jnp.where(hit, prob_t[k][None, :], prob)
    return named, prob


def along_z(rows, depth):
    up = [(i, (i + 1) % depth) for i in range(depth)]
    down = [(i, (i - 1) % depth) for i in range(depth)]
    below = above = rows
    blocks, offsets = [rows], [0]
    for step in range(1, depth // 2 + 1):
        below = lax.ppermute(below, "z", up)
        blocks.append(below)
        offsets.append(depth - step)
        if step < depth - step:
            above = lax.ppermute(above, "z", down)
            blocks.append(above)
            offsets.append(step)
    return blocks, offsets


def iota(shape, dim):
    return lax.broadcasted_iota(jnp.int32, shape, dim)


def prepare(x, ids_t, prob_t):
    toks, width = x.shape
    top = ids_t.shape[0]

    def body(x_ref, ids_ref, prob_ref, out_ref):
        out_ref[:, :width] = x_ref[...].astype(BF16)
        small = jnp.concatenate([ids_ref[...].astype(F32), prob_ref[...]], axis=0).astype(BF16)
        place = (iota((2 * top, LANES), 0) == iota((2 * top, LANES), 1)).astype(F32).astype(BF16)
        out_ref[:, width:] = mm(small, place, ((0,), (0,))).astype(BF16)

    return pl.pallas_call(
        body,
        out_specs=IN_VMEM,
        out_shape=jax.ShapeDtypeStruct((toks, width + LANES), BF16),
        name="prepare",
    )(x, ids_t, prob_t)


def narrow(x, after):
    def body(x_ref, *refs):
        refs[-1][...] = x_ref[...].astype(BF16)

    return pl.pallas_call(
        body,
        in_specs=[IN_VMEM] * (1 + len(after)),
        out_specs=IN_VMEM,
        out_shape=jax.ShapeDtypeStruct(x.shape, BF16),
        compiler_params=pltpu.CompilerParams(vmem_limit_bytes=SCOPED),
        name="narrow",
    )(x, *after)


def fill_x(blocks, offsets, z, top, cap, width, parts, after):
    toks = blocks[0].shape[0]
    depth = len(blocks)
    cols = depth * toks
    rows = depth * cap
    slots = PLANE * rows
    chunk = width // parts

    def body(z_ref, *refs):
        out_ref, weigh_ref, pick_ref, buf_ref, sems = refs[depth + len(after) :]
        refs = refs[:depth]
        if True:
            me = z_ref[0]
            meta = jnp.concatenate([ref[:, width:] for ref in refs], axis=0)
            take = (iota((2 * top, LANES), 0) == iota((2 * top, LANES), 1)).astype(F32).astype(BF16)
            small = mm(take, meta, ((1,), (1,)))
            expert = (iota((PLANE, cols), 0) + me * PLANE).astype(F32)
            named = jnp.zeros((PLANE, cols), F32)
            prob = jnp.zeros((PLANE, cols), F32)
            for k in range(top):
                hit = small[k : k + 1] == expert
                named = jnp.where(hit, 1.0, named)
                prob = jnp.where(hit, small[top + k : top + k + 1], prob)
            i, j = iota((cols, cols), 0), iota((cols, cols), 1)
            start = jnp.zeros((cols, cols), jnp.int32)
            for b in range(1, depth):
                start = jnp.where(j >= b * toks, b * toks, start)
            earlier = jnp.where((i < j) & (i >= start), 1.0, 0.0).astype(BF16)
            rank = mm(named.astype(BF16), earlier, ((1,), (0,)))
            rank = jnp.where(named > 0.0, rank, -64.0 * depth)
            row, col = iota((rows, cols), 0), iota((rows, cols), 1)
            source = jnp.zeros((rows, cols), jnp.int32)
            for b in range(depth):
                source = jnp.where(col >= b * toks, (me + offsets[b]) & (depth - 1), source)
            wanted = (row - source * cap).astype(F32)
            for e in range(PLANE):
                chosen = (rank[e : e + 1] == wanted)
                pick_ref[e * rows : (e + 1) * rows] = jnp.where(chosen, 1.0, 0.0).astype(BF16)
                weigh_ref[e * rows : (e + 1) * rows] = jnp.where(chosen, prob[e : e + 1], 0.0).astype(BF16)

        def send(i):
            here = pl.ds(i, chunk)
            return pltpu.make_async_copy(buf_ref.at[:, here], out_ref.at[:, here], sems.at[i // chunk])

        for i in range(0, width, chunk):
            x = jnp.concatenate([ref[:, i : i + chunk] for ref in refs], axis=0)
            buf_ref[:, i : i + chunk] = mm(pick_ref[...], x, ((1,), (0,))).astype(BF16)
            send(i).start()
        for i in range(0, width, chunk):
            send(i).wait()

    return pl.pallas_call(
        body,
        in_specs=[pl.BlockSpec(memory_space=pltpu.SMEM)] + [IN_VMEM] * (depth + len(after)),
        out_specs=[IN_HBM, IN_VMEM],
        scratch_shapes=[
            pltpu.VMEM((slots, cols), BF16),
            pltpu.VMEM((slots, width), BF16),
            pltpu.SemaphoreType.DMA((parts,)),
        ],
        out_shape=[pltpu.HBM((slots, width), BF16), pltpu.VMEM((slots, cols), BF16)],
        compiler_params=pltpu.CompilerParams(vmem_limit_bytes=SCOPED),
        name="fill_x",
    )(z, *blocks, *after)


def fill_g(weigh, blocks, parts):
    toks, width = blocks[0].shape
    slots, cols = weigh.shape
    chunk = width // parts

    def body(weigh_ref, *refs):
        refs, (out_ref, buf_ref, sems) = refs[:-3], refs[-3:]

        def send(i):
            here = pl.ds(i, chunk)
            return pltpu.make_async_copy(buf_ref.at[:, here], out_ref.at[:, here], sems.at[i // chunk])

        for i in range(0, width, chunk):
            g = jnp.concatenate([ref[:, i : i + chunk] for ref in refs], axis=0)
            buf_ref[:, i : i + chunk] = mm(weigh_ref[...], g, ((1,), (0,))).astype(BF16)
            send(i).start()
        for i in range(0, width, chunk):
            send(i).wait()

    return pl.pallas_call(
        body,
        in_specs=[IN_VMEM] * (1 + len(blocks)),
        out_specs=IN_HBM,
        scratch_shapes=[pltpu.VMEM((slots, width), BF16), pltpu.SemaphoreType.DMA((parts,))],
        out_shape=pltpu.HBM((slots, width), BF16),
        compiler_params=pltpu.CompilerParams(vmem_limit_bytes=SCOPED),
        name="fill_g",
    )(weigh, *blocks)


def activations(xs, wg, wu, part):
    rows, width = xs.shape
    hidden = wg.shape[1]

    def body(x_h, wg_ref, wu_ref, act_h, slope_h, hid_h, act_ref, slope_ref, hid_ref, x_ref, sems):
        arrive = pltpu.make_async_copy(x_h, x_ref, sems.at[3])
        arrive.start()
        arrive.wait()
        for i in range(0, hidden, part):
            a = mm(x_ref[...], wg_ref[:, i : i + part], ((1,), (0,)))
            b = mm(x_ref[...], wu_ref[:, i : i + part], ((1,), (0,)))
            sig = 1.0 / (1.0 + jnp.exp(-a))
            act = a * sig
            act_ref[:, i : i + part] = act
            slope_ref[:, i : i + part] = b * sig * (1.0 + a * (1.0 - sig))
            hid_ref[:, i : i + part] = (act * b).astype(BF16)
        copies = [
            pltpu.make_async_copy(src, dst, sems.at[i])
            for i, (src, dst) in enumerate([(act_ref, act_h), (slope_ref, slope_h), (hid_ref, hid_h)])
        ]
        for copy in copies:
            copy.start()
        for copy in copies:
            copy.wait()

    return pl.pallas_call(
        body,
        in_specs=[IN_HBM, IN_VMEM, IN_VMEM],
        out_specs=[IN_HBM] * 3,
        out_shape=[
            pltpu.HBM((rows, hidden), F32),
            pltpu.HBM((rows, hidden), F32),
            pltpu.HBM((rows, hidden), BF16),
        ],
        scratch_shapes=[
            pltpu.VMEM((rows, hidden), F32),
            pltpu.VMEM((rows, hidden), F32),
            pltpu.VMEM((rows, hidden), BF16),
            pltpu.VMEM((rows, width), BF16),
            pltpu.SemaphoreType.DMA((4,)),
        ],
        compiler_params=pltpu.CompilerParams(vmem_limit_bytes=2 * SCOPED),
        name="activations",
    )(pltpu.with_memory_space_constraint(xs, pltpu.HBM), wg, wu)


def combine(pick, rows, parts):
    slots, toks = pick.shape
    peers, cap, width = rows.shape
    chunk = width // parts

    def body(pick_ref, rows_ref, out_ref):
        for i in range(0, width, chunk):
            part = rows_ref[:, :, i : i + chunk].astype(F32).reshape(slots, chunk).astype(BF16)
            out_ref[:, i : i + chunk] = mm(pick_ref[...], part, ((0,), (0,)))

    return pl.pallas_call(
        body,
        in_specs=[IN_VMEM, IN_VMEM],
        out_shape=jax.ShapeDtypeStruct((toks, width), F32),
        compiler_params=pltpu.CompilerParams(vmem_limit_bytes=SCOPED),
        name="combine",
    )(pick, rows)


def backward(go, wd, act, slope, wg, wu, part, parts, cap):
    rows, width = go.shape
    hidden = wd.shape[1]
    chunk = width // parts
    shape = (rows // cap, cap, width)

    def body(go_h, wd_h, act_h, slope_h, wg_h, wu_h, dxs_h, da_h, db_h, *scratch):
        go_ref, wd_ref, act_ref, slope_ref, wg_ref, wu_ref, dxs_ref, da_ref, db_ref, sems = scratch
        steps = hidden // part

        def load(n, src, dst):
            return pltpu.make_async_copy(src, dst, sems.at[n])

        def columns(n):
            here = pl.ds(n * part, part)
            return load(8 + n, wd_h.at[:, here], wd_ref.at[:, here])

        wd_in = [columns(n) for n in range(steps)]
        go_in, slope_in, act_in = load(0, go_h, go_ref), load(1, slope_h, slope_ref), load(2, act_h, act_ref)
        later = [load(3, wg_h, wg_ref), load(4, wu_h, wu_ref)]
        keep = [load(5, da_ref, da_h), load(6, db_ref, db_h)]

        def send(i):
            here = pl.ds(i, chunk)
            return pltpu.make_async_copy(
                dxs_ref.at[:, :, here], dxs_h.at[:, :, here], sems.at[8 + steps + i // chunk]
            )

        go_in.start()
        wd_in[0].start()
        slope_in.start()
        act_in.start()
        go_in.wait()
        wd_in[0].wait()
        for copy in wd_in[1:] + later:
            copy.start()
        slope_in.wait()
        act_in.wait()
        for i in range(0, hidden, part):
            if i > 0:
                wd_in[i // part].wait()
            dh = mm(go_ref[...], wd_ref[:, i : i + part], ((1,), (0,)))
            da_ref[:, i : i + part] = (dh * slope_ref[:, i : i + part]).astype(BF16)
            db_ref[:, i : i + part] = (dh * act_ref[:, i : i + part]).astype(BF16)
        for copy in later:
            copy.wait()
        for i in range(0, width, chunk):
            dxs = mm(da_ref[...], wg_ref[i : i + chunk, :], ((1,), (1,))) + mm(
                db_ref[...], wu_ref[i : i + chunk, :], ((1,), (1,))
            )
            dxs_ref[:, :, i : i + chunk] = dxs.reshape(shape[0], cap, chunk).astype(BF16)
            send(i).start()
        for copy in keep:
            copy.start()
        for i in range(0, width, chunk):
            send(i).wait()
        for copy in keep:
            copy.wait()

    return pl.pallas_call(
        body,
        in_specs=[IN_HBM] * 6,
        out_specs=[IN_HBM] * 3,
        out_shape=[
            pltpu.HBM(shape, BF16),
            pltpu.HBM((rows, hidden), BF16),
            pltpu.HBM((rows, hidden), BF16),
        ],
        scratch_shapes=[
            pltpu.VMEM((rows, width), BF16),
            pltpu.VMEM((width, hidden), BF16),
            pltpu.VMEM((rows, hidden), F32),
            pltpu.VMEM((rows, hidden), F32),
            pltpu.VMEM((width, hidden), BF16),
            pltpu.VMEM((width, hidden), BF16),
            pltpu.VMEM(shape, BF16),
            pltpu.VMEM((rows, hidden), BF16),
            pltpu.VMEM((rows, hidden), BF16),
            pltpu.SemaphoreType.DMA((8 + hidden // part + parts,)),
        ],
        compiler_params=pltpu.CompilerParams(vmem_limit_bytes=4 * SCOPED),
        name="backward",
    )(*(pltpu.with_memory_space_constraint(v, pltpu.HBM) for v in (go, wd, act, slope, wg, wu)))


def per_device(hidden_in, out_grad, route_prob, route_ids, w_gate, w_up, w_down):
    tok_count, top_count = route_ids.shape
    width = hidden_in.shape[1]
    depth = lax.axis_size("z")
    peers = depth * PLANE
    half = w_gate.shape[2]
    slot_cap = max(2, 12 * tok_count // peers)
    total_slots = peers * slot_cap
    swap = [(0, 1), (1, 0)]

    column, came_from = along_z(prepare(hidden_in, route_ids.T, route_prob.T), depth)
    g_column, _ = along_z(narrow(out_grad, column[-3:-1]), depth)
    block = depth * slot_cap
    send_x, weigh = fill_x(
        column, came_from, lax.axis_index("z").reshape(1), top_count, slot_cap, width, 4, g_column[1:3]
    )

    def in_plane(rows):
        return lax.all_to_all(
            rows.reshape(PLANE, block, width), ("y", "x"), split_axis=0, concat_axis=0, tiled=True
        ).reshape(total_slots, width)

    xs = in_plane(send_x)
    send_g = fill_g(weigh, g_column, 4)
    send_g, xs = lax.optimization_barrier((send_g, xs))
    go = in_plane(send_g)

    slot = lax.broadcasted_iota(jnp.int32, (total_slots, 1), 0)
    peer = slot // slot_cap
    slot_expert = (peer % depth) * PLANE + peer // depth
    named, _ = named_by(slot_expert, route_ids.T, None)
    rank = mm(named.astype(BF16), before(tok_count, tok_count), ((1,), (0,)))
    pick = ((named > 0.0) & (rank == (slot % slot_cap).astype(F32))).astype(BF16)

    def both(w):
        return jnp.concatenate([w[0], lax.ppermute(w[0], "dp", swap)], axis=1)

    wg, wu, wd = both(w_gate), both(w_up), both(w_down)

    act, slope, hid = activations(xs, wg, wu, 256)
    dxs, da, db = backward(go, wd, act, slope, wg, wu, 256, 4, slot_cap)
    returned = lax.all_to_all(dxs, ("y", "x", "z"), split_axis=0, concat_axis=0, tiled=True)

    def grad(rows, hidden):
        mine = mm(rows, hidden[:, :half], ((0,), (0,))).astype(BF16)
        other = mm(rows, hidden[:, half:], ((0,), (0,))).astype(BF16)
        got = lax.ppermute(other, "dp", swap)
        return (mine.astype(F32) + got.astype(F32)).astype(BF16)[None]

    grads = (grad(xs, da), grad(xs, db), grad(go, hid))
    input_grad = combine(pick, returned, 4)
    return (input_grad, grads[0], grads[1], grads[2])


def solution(mesh):
    grid = Mesh(mesh.devices.reshape(-1, 4, 4, 2), ("z", "y", "x", "dp"))
    tok = P(("z", "y", "x", "dp"), None)
    wts = P(("z", "y", "x"), None, "dp")
    return jax.shard_map(
        per_device,
        mesh=grid,
        in_specs=(tok, tok, tok, tok, wts, wts, wts),
        out_specs=(tok, wts, wts, wts),
        check_vma=False,
    )
```

profile of v0, /device:TPU:32, one launch (start us, length us, event | category | flops | bytes accessed | tf_op | source)
XLA Modules:
  0.0 187.4 jit_solution(13854111883162283886)
XLA Ops:
  0.6 1.9 prepare.1.refs_0_
  2.5 1.9 %collective-permute-start = (bf16[48,2176]{1,0:T(8,128)(2,1)}, bf16[48,2176]{1,0:T(8,128)(2,1)S(1)}, u32[]{:S(2)}, u32[]{:S(2)}) collective-permute-start(bf16[48,2176]{1,0:T(8,128)(2,1)} %prepare.1.refs_0_), channel_id=1, source_target_pairs={{0,32},{32,64},{64,96},{96,128},{128,160},{160,192},{192,224},{224... | collective-permute-start | bytes 626696 | tf_op jit(solution)/shard_map/ppermute | solution.py:44
  4.5 5.1 %collective-permute-done.refs_1_ = bf16[48,2176]{1,0:T(8,128)(2,1)S(1)} collective-permute-done((bf16[48,2176]{1,0:T(8,128)(2,1)}, bf16[48,2176]{1,0:T(8,128)(2,1)S(1)}, u32[]{:S(2)}, u32[]{:S(2)}) %collective-permute-start) | collective-permute-done | bytes 208928 | tf_op jit(solution)/shard_map/ppermute | solution.py:44
  9.6 1.9 %collective-permute-start.2 = (bf16[48,2176]{1,0:T(8,128)(2,1)S(1)}, bf16[48,2176]{1,0:T(8,128)(2,1)S(1)}, u32[]{:S(2)}, u32[]{:S(2)}) collective-permute-start(bf16[48,2176]{1,0:T(8,128)(2,1)S(1)} %collective-permute-done.refs_1_), channel_id=1, source_target_pairs={{0,32},{32,64},{64,96},{96,128},{128,160},{160,192},{192,224},{224... | collective-permute-start | bytes 626696 | tf_op jit(solution)/shard_map/ppermute | solution.py:44
  11.5 2.3 %collective-permute-start.3 = (bf16[48,2176]{1,0:T(8,128)(2,1)S(1)}, bf16[48,2176]{1,0:T(8,128)(2,1)S(1)}, u32[]{:S(2)}, u32[]{:S(2)}) collective-permute-start(bf16[48,2176]{1,0:T(8,128)(2,1)S(1)} %collective-permute-done.1.refs_2_), channel_id=1, source_target_pairs={{0,224},{32,0},{64,32},{96,64},{128,96},{160,128},{192,160},{224,1... | collective-permute-start | bytes 626696 | tf_op jit(solution)/shard_map/ppermute | solution.py:48
  13.9 4.6 %collective-permute-done.2.refs_3_ = bf16[48,2176]{1,0:T(8,128)(2,1)S(1)} collective-permute-done((bf16[48,2176]{1,0:T(8,128)(2,1)S(1)}, bf16[48,2176]{1,0:T(8,128)(2,1)S(1)}, u32[]{:S(2)}, u32[]{:S(2)}) %collective-permute-start.2) | collective-permute-done | bytes 208928 | tf_op jit(solution)/shard_map/ppermute | solution.py:44
  18.5 0.4 collective-permute-done.3.refs_4_
  18.9 2.5 %collective-permute-start.5 = (bf16[48,2176]{1,0:T(8,128)(2,1)S(1)}, bf16[48,2176]{1,0:T(8,128)(2,1)S(1)}, u32[]{:S(2)}, u32[]{:S(2)}) collective-permute-start(bf16[48,2176]{1,0:T(8,128)(2,1)S(1)} %collective-permute-done.3.refs_4_), channel_id=1, source_target_pairs={{0,224},{32,0},{64,32},{96,64},{128,96},{160,128},{192,160},{224,1... | collective-permute-start | bytes 626696 | tf_op jit(solution)/shard_map/ppermute | solution.py:48
  21.4 3.8 %collective-permute-done.4.refs_0_.refs_5_ = bf16[48,2176]{1,0:T(8,128)(2,1)S(1)} collective-permute-done((bf16[48,2176]{1,0:T(8,128)(2,1)S(1)}, bf16[48,2176]{1,0:T(8,128)(2,1)S(1)}, u32[]{:S(2)}, u32[]{:S(2)}) %collective-permute-start.4) | collective-permute-done | bytes 208928 | tf_op jit(solution)/shard_map/ppermute | solution.py:44
  25.6 1.0 copy-done.3
  26.6 2.9 %collective-permute-start.8 = (bf16[48,2048]{1,0:T(8,128)(2,1)S(1)}, bf16[48,2048]{1,0:T(8,128)(2,1)S(1)}, u32[]{:S(2)}, u32[]{:S(2)}) collective-permute-start(bf16[48,2048]{1,0:T(8,128)(2,1)S(1)} %narrow.1.refs_0_), channel_id=1, source_target_pairs={{0,224},{32,0},{64,32},{96,64},{128,96},{160,128},{192,160},{224,1... | collective-permute-start | bytes 589832 | tf_op jit(solution)/shard_map/ppermute | solution.py:48
  29.5 0.5 collective-permute-start.7
  30.0 3.6 %collective-permute-done.8.refs_9_.refs_2_ = bf16[48,2048]{1,0:T(8,128)(2,1)S(1)} collective-permute-done((bf16[48,2048]{1,0:T(8,128)(2,1)S(1)}, bf16[48,2048]{1,0:T(8,128)(2,1)S(1)}, u32[]{:S(2)}, u32[]{:S(2)}) %collective-permute-start.8) | collective-permute-done | bytes 196640 | tf_op jit(solution)/shard_map/ppermute | solution.py:48
  33.6 2.8 %collective-permute-done.7.refs_8_.refs_1_ = bf16[48,2048]{1,0:T(8,128)(2,1)S(1)} collective-permute-done((bf16[48,2048]{1,0:T(8,128)(2,1)S(1)}, bf16[48,2048]{1,0:T(8,128)(2,1)S(1)}, u32[]{:S(2)}, u32[]{:S(2)}) %collective-permute-start.7) | collective-permute-done | bytes 196640 | tf_op jit(solution)/shard_map/ppermute | solution.py:44
  36.4 0.9 copy-done.2
  37.3 2.5 %fill_x.1 = (bf16[512,2048]{1,0:T(8,128)(2,1)}, bf16[512,384]{1,0:T(8,128)(2,1)S(1)}) custom-call(s32[1]{0:T(128)} %bitcast.9.z_ref, bf16[48,2176]{1,0:T(8,128)(2,1)S(1)} %copy-done.2, bf16[48,2176]{1,0:T(8,128)(2,1)S(1)} %collective-permute-done.refs_1_, bf16[48,2176]{1,0:T(8,128)(2,1)S(1)} %collective-permute-done.1.refs_2_, ...), custom_call_target="tpu_custom_call" | custom-call | tf_op jit(solution)/shard_map/fill_x/pallas_call | solution.py:141
  39.8 7.0 %all-to-all-start = ((bf16[16,32,2048]{2,1,0:T(8,128)(2,1)}), bf16[16,32,2048]{2,1,0:T(8,128)(2,1)S(1)}, u32[]{:S(2)}, u32[]{:S(2)}) async-start(bf16[16,32,2048]{2,1,0:T(8,128)(2,1)} %bitcast.47), calls=%async_computation | async-start | bytes 4194304 | tf_op jit(solution)/shard_map/all_to_all | solution.py:354
  46.9 0.5 collective-permute-start.9
  47.4 3.0 %collective-permute-start.10 = (bf16[48,2048]{1,0:T(8,128)(2,1)S(1)}, bf16[48,2048]{1,0:T(8,128)(2,1)S(1)}, u32[]{:S(2)}, u32[]{:S(2)}) collective-permute-start(bf16[48,2048]{1,0:T(8,128)(2,1)S(1)} %collective-permute-done.8.refs_9_.refs_2_), channel_id=1, source_target_pairs={{0,224},{32,0},{64,32},{96,64},{128,96},{160,128},{192,160},{224,1... | collective-permute-start | bytes 589832 | tf_op jit(solution)/shard_map/ppermute | solution.py:48
  50.4 3.5 %collective-permute-done.9.refs_3_ = bf16[48,2048]{1,0:T(8,128)(2,1)S(1)} collective-permute-done((bf16[48,2048]{1,0:T(8,128)(2,1)S(1)}, bf16[48,2048]{1,0:T(8,128)(2,1)S(1)}, u32[]{:S(2)}, u32[]{:S(2)}) %collective-permute-start.9) | collective-permute-done | bytes 196640 | tf_op jit(solution)/shard_map/ppermute | solution.py:44
  53.8 2.3 %collective-permute-done.10.refs_4_ = bf16[48,2048]{1,0:T(8,128)(2,1)S(1)} collective-permute-done((bf16[48,2048]{1,0:T(8,128)(2,1)S(1)}, bf16[48,2048]{1,0:T(8,128)(2,1)S(1)}, u32[]{:S(2)}, u32[]{:S(2)}) %collective-permute-start.10) | collective-permute-done | bytes 196640 | tf_op jit(solution)/shard_map/ppermute | solution.py:48
  56.2 2.1 %collective-permute-start.12 = (bf16[48,2048]{1,0:T(8,128)(2,1)S(1)}, bf16[48,2048]{1,0:T(8,128)(2,1)S(1)}, u32[]{:S(2)}, u32[]{:S(2)}) collective-permute-start(bf16[48,2048]{1,0:T(8,128)(2,1)S(1)} %collective-permute-done.10.refs_4_), channel_id=1, source_target_pairs={{0,224},{32,0},{64,32},{96,64},{128,96},{160,128},{192,160},{224,1... | collective-permute-start | bytes 589832 | tf_op jit(solution)/shard_map/ppermute | solution.py:48
  58.3 2.5 %collective-permute-done.11.refs_5_ = bf16[48,2048]{1,0:T(8,128)(2,1)S(1)} collective-permute-done((bf16[48,2048]{1,0:T(8,128)(2,1)S(1)}, bf16[48,2048]{1,0:T(8,128)(2,1)S(1)}, u32[]{:S(2)}, u32[]{:S(2)}) %collective-permute-start.11) | collective-permute-done | bytes 196640 | tf_op jit(solution)/shard_map/ppermute | solution.py:44
  60.7 3.7 %collective-permute-done.12.refs_6_ = bf16[48,2048]{1,0:T(8,128)(2,1)S(1)} collective-permute-done((bf16[48,2048]{1,0:T(8,128)(2,1)S(1)}, bf16[48,2048]{1,0:T(8,128)(2,1)S(1)}, u32[]{:S(2)}, u32[]{:S(2)}) %collective-permute-start.12) | collective-permute-done | bytes 196640 | tf_op jit(solution)/shard_map/ppermute | solution.py:48
  64.4 3.2 %collective-permute-done.13.refs_7_ = bf16[48,2048]{1,0:T(8,128)(2,1)S(1)} collective-permute-done((bf16[48,2048]{1,0:T(8,128)(2,1)S(1)}, bf16[48,2048]{1,0:T(8,128)(2,1)S(1)}, u32[]{:S(2)}, u32[]{:S(2)}) %collective-permute-start.13) | collective-permute-done | bytes 196640 | tf_op jit(solution)/shard_map/ppermute | solution.py:44
  67.6 2.1 %fill_g.1 = bf16[512,2048]{1,0:T(8,128)(2,1)} custom-call(bf16[512,384]{1,0:T(8,128)(2,1)S(1)} %get-tuple-element.14.weigh_ref, bf16[48,2048]{1,0:T(8,128)(2,1)S(1)} %narrow.1.refs_0_, bf16[48,2048]{1,0:T(8,128)(2,1)S(1)} %collective-permute-done.7.refs_8_.refs_1_, bf16[48,2048]{1,0:T(8,128)(2,1)S(1)} %collective-permute-done.8.refs_9_.refs_2_, ...), custom_call_target="tpu_custom_call" | custom-call | tf_op jit(solution)/shard_map/fill_g/pallas_call | solution.py:175
  69.7 5.1 %all-to-all-done = bf16[16,32,2048]{2,1,0:T(8,128)(2,1)S(1)} async-done(((bf16[16,32,2048]{2,1,0:T(8,128)(2,1)}), bf16[16,32,2048]{2,1,0:T(8,128)(2,1)S(1)}, u32[]{:S(2)}, u32[]{:S(2)}) %all-to-all-start) | async-done | bytes 2097184 | tf_op jit(solution)/shard_map/all_to_all | solution.py:354
  74.8 1.3 copy-done.6
  76.1 3.7 %all-to-all-start.1 = ((bf16[16,32,2048]{2,1,0:T(8,128)(2,1)}), bf16[16,32,2048]{2,1,0:T(8,128)(2,1)S(1)}, u32[]{:S(2)}, u32[]{:S(2)}) async-start(bf16[16,32,2048]{2,1,0:T(8,128)(2,1)} %bitcast.41), calls=%async_computation.1 | async-start | bytes 4194304 | tf_op jit(solution)/shard_map/all_to_all | solution.py:354
  80.0 2.2 %pad_maximum_fusion.1.wg_ref.wg_h = bf16[2048,768]{1,0:T(8,128)(2,1)S(1)} fusion(bf16[2048,384]{1,0:T(8,128)(2,1)} %collective-permute-done.15, bf16[2048,384]{1,0:T(8,128)(2,1)} %bitcast.49), kind=kLoop, calls=%fused_computation.1 | loop fusion | flops 6291456 | bytes 6291456 | tf_op jit(solution)/shard_map/concatenate | solution.py:371
  82.3 2.8 %pad_maximum_fusion.2.wu_ref.wu_h = bf16[2048,768]{1,0:T(8,128)(2,1)S(1)} fusion(bf16[2048,384]{1,0:T(8,128)(2,1)} %collective-permute-done.16, bf16[2048,384]{1,0:T(8,128)(2,1)S(1)} %bitcast.51), kind=kLoop, calls=%fused_computation.2 | loop fusion | flops 6291456 | bytes 6291456 | tf_op jit(solution)/shard_map/concatenate | solution.py:371
  85.2 2.3 %pad_maximum_fusion.wd_h = bf16[2048,768]{1,0:T(8,128)(2,1)} fusion(bf16[2048,384]{1,0:T(8,128)(2,1)S(1)} %collective-permute-done.14, bf16[2048,384]{1,0:T(8,128)(2,1)S(1)} %bitcast.53), kind=kLoop, calls=%fused_computation | loop fusion | flops 6291456 | bytes 6291456 | tf_op jit(solution)/shard_map/concatenate | solution.py:371
  87.8 7.3 %activations.1 = (f32[512,768]{1,0:T(8,128)}, f32[512,768]{1,0:T(8,128)}, bf16[512,768]{1,0:T(8,128)(2,1)}) custom-call(bf16[512,2048]{1,0:T(8,128)(2,1)} %bitcast.42, bf16[2048,768]{1,0:T(8,128)(2,1)S(1)} %pad_maximum_fusion.1.wg_ref.wg_h, bf16[2048,768]{1,0:T(8,128)(2,1)S(1)} %pad_maximum_fusion.2.wu_ref.wu_h), custom_call_target="tpu_custom_call" | custom-call | tf_op jit(solution)/shard_map/activations/pallas_call | solution.py:211
  95.1 14.4 %all-to-all-done.1 = bf16[16,32,2048]{2,1,0:T(8,128)(2,1)S(1)} async-done(((bf16[16,32,2048]{2,1,0:T(8,128)(2,1)}), bf16[16,32,2048]{2,1,0:T(8,128)(2,1)S(1)}, u32[]{:S(2)}, u32[]{:S(2)}) %all-to-all-start.1) | async-done | bytes 2097184 | tf_op jit(solution)/shard_map/all_to_all | solution.py:354
  109.5 1.4 copy-done.4
  110.8 11.3 %backward.1 = (bf16[128,4,2048]{2,1,0:T(4,128)(2,1)}, bf16[512,768]{1,0:T(8,128)(2,1)}, bf16[512,768]{1,0:T(8,128)(2,1)}) custom-call(bf16[512,2048]{1,0:T(8,128)(2,1)} %bitcast.38, bf16[2048,768]{1,0:T(8,128)(2,1)} %pad_maximum_fusion.wd_h, f32[512,768]{1,0:T(8,128)} %get-tuple-element.18.act_h, f32[512,768]{1,0:T(8,128)} %get-tuple-element.19.slope_h, ...), custom_call_target="tpu_custom_call" | custom-call | tf_op jit(solution)/shard_map/backward/pallas_call | solution.py:310
  122.2 10.0 %all-to-all-start.2 = ((bf16[128,4,2048]{2,1,0:T(4,128)(2,1)}), bf16[128,4,2048]{2,1,0:T(4,128)(2,1)S(1)}, u32[]{:S(2)}, u32[]{:S(2)}) async-start(bf16[128,4,2048]{2,1,0:T(4,128)(2,1)} %get-tuple-element.20), calls=%async_computation.2 | async-start | bytes 4194304 | tf_op jit(solution)/shard_map/all_to_all | solution.py:377
  132.2 3.0 %convolution_convert_fusion = bf16[2048,384]{1,0:T(8,128)(2,1)S(1)} fusion(bf16[512,2048]{1,0:T(8,128)(2,1)} %bitcast.39, bf16[512,768]{1,0:T(8,128)(2,1)S(1)} %copy-done.12), kind=kOutput, calls=%fused_computation.6 | convolution fusion | flops 806092800 | bytes 4063232 | tf_op jit(solution)/shard_map/dot_general | solution.py:18
  135.4 1.3 convolution_convert_fusion.2
  136.7 0.6 collective-permute-start.18
  137.3 1.3 convolution_convert_fusion.4
  138.7 0.4 fusion.4.pick_ref
  139.2 1.0 copy-done.5
  140.1 2.5 %fusion.2 = bf16[1,2048,384]{2,1,0:T(8,128)(2,1)} fusion(bf16[2048,384]{1,0:T(8,128)(2,1)S(1)} %collective-permute-done.19, bf16[512,2048]{1,0:T(8,128)(2,1)S(1)} %bitcast.40, bf16[512,768]{1,0:T(8,128)(2,1)S(1)} %copy-done.12), kind=kOutput, calls=%fused_computation.14 | convolution fusion | flops 809238528 | bytes 5636096 | tf_op jit(solution)/shard_map/dot_general | solution.py:18
  142.6 2.5 %fusion.1 = bf16[1,2048,384]{2,1,0:T(8,128)(2,1)} fusion(bf16[2048,384]{1,0:T(8,128)(2,1)S(1)} %collective-permute-done.18, bf16[512,2048]{1,0:T(8,128)(2,1)S(1)} %bitcast.45, bf16[512,768]{1,0:T(8,128)(2,1)S(1)} %copy-done.13), kind=kOutput, calls=%fused_computation.13 | convolution fusion | flops 809238528 | bytes 5636096 | tf_op jit(solution)/shard_map/dot_general | solution.py:18
  145.1 2.5 %fusion = bf16[1,2048,384]{2,1,0:T(8,128)(2,1)} fusion(bf16[2048,384]{1,0:T(8,128)(2,1)S(1)} %collective-permute-done.17, bf16[512,2048]{1,0:T(8,128)(2,1)S(1)} %bitcast.46, bf16[512,768]{1,0:T(8,128)(2,1)S(1)} %copy-done.11), kind=kOutput, calls=%fused_computation.12 | convolution fusion | flops 809238528 | bytes 5636096 | tf_op jit(solution)/shard_map/dot_general | solution.py:18
  147.6 38.5 %all-to-all-done.2.rows_ref = bf16[128,4,2048]{2,1,0:T(4,128)(2,1)S(1)} async-done(((bf16[128,4,2048]{2,1,0:T(4,128)(2,1)}), bf16[128,4,2048]{2,1,0:T(4,128)(2,1)S(1)}, u32[]{:S(2)}, u32[]{:S(2)}) %all-to-all-start.2) | async-done | bytes 2097184 | tf_op jit(solution)/shard_map/all_to_all | solution.py:377
  186.1 1.3 combine.1
  (47 shorter events, 1.4 us)
Async XLA Ops:
  2.5 7.1 %collective-permute-start = (bf16[48,2176]{1,0:T(8,128)(2,1)}, bf16[48,2176]{1,0:T(8,128)(2,1)S(1)}, u32[]{:S(2)}, u32[]{:S(2)}) collective-permute-start(bf16[48,2176]{1,0:T(8,128)(2,1)} %prepare.1.refs_0_), channel_id=1, source_target_pairs={{0,32},{32,64},{64,96},{96,128},{128,160},{160,192},{192,224},{224... | collective-permute-start | bytes 626696 | tf_op jit(solution)/shard_map/ppermute | solution.py:44
  4.4 7.1 %collective-permute-start.1 = (bf16[48,2176]{1,0:T(8,128)(2,1)}, bf16[48,2176]{1,0:T(8,128)(2,1)S(1)}, u32[]{:S(2)}, u32[]{:S(2)}) collective-permute-start(bf16[48,2176]{1,0:T(8,128)(2,1)} %prepare.1.refs_0_), channel_id=1, source_target_pairs={{0,224},{32,0},{64,32},{96,64},{128,96},{160,128},{192,160},{224,1... | collective-permute-start | bytes 626696 | tf_op jit(solution)/shard_map/ppermute | solution.py:48
  9.6 8.8 %collective-permute-start.2 = (bf16[48,2176]{1,0:T(8,128)(2,1)S(1)}, bf16[48,2176]{1,0:T(8,128)(2,1)S(1)}, u32[]{:S(2)}, u32[]{:S(2)}) collective-permute-start(bf16[48,2176]{1,0:T(8,128)(2,1)S(1)} %collective-permute-done.refs_1_), channel_id=1, source_target_pairs={{0,32},{32,64},{64,96},{96,128},{128,160},{160,192},{192,224},{224... | collective-permute-start | bytes 626696 | tf_op jit(solution)/shard_map/ppermute | solution.py:44
  11.5 7.3 %collective-permute-start.3 = (bf16[48,2176]{1,0:T(8,128)(2,1)S(1)}, bf16[48,2176]{1,0:T(8,128)(2,1)S(1)}, u32[]{:S(2)}, u32[]{:S(2)}) collective-permute-start(bf16[48,2176]{1,0:T(8,128)(2,1)S(1)} %collective-permute-done.1.refs_2_), channel_id=1, source_target_pairs={{0,224},{32,0},{64,32},{96,64},{128,96},{160,128},{192,160},{224,1... | collective-permute-start | bytes 626696 | tf_op jit(solution)/shard_map/ppermute | solution.py:48
  18.5 6.7 %collective-permute-start.4 = (bf16[48,2176]{1,0:T(8,128)(2,1)S(1)}, bf16[48,2176]{1,0:T(8,128)(2,1)S(1)}, u32[]{:S(2)}, u32[]{:S(2)}) collective-permute-start(bf16[48,2176]{1,0:T(8,128)(2,1)S(1)} %collective-permute-done.2.refs_3_), channel_id=1, source_target_pairs={{0,32},{32,64},{64,96},{96,128},{128,160},{160,192},{192,224},{224... | collective-permute-start | bytes 626696 | tf_op jit(solution)/shard_map/ppermute | solution.py:44
  18.9 6.7 %collective-permute-start.5 = (bf16[48,2176]{1,0:T(8,128)(2,1)S(1)}, bf16[48,2176]{1,0:T(8,128)(2,1)S(1)}, u32[]{:S(2)}, u32[]{:S(2)}) collective-permute-start(bf16[48,2176]{1,0:T(8,128)(2,1)S(1)} %collective-permute-done.3.refs_4_), channel_id=1, source_target_pairs={{0,224},{32,0},{64,32},{96,64},{128,96},{160,128},{192,160},{224,1... | collective-permute-start | bytes 626696 | tf_op jit(solution)/shard_map/ppermute | solution.py:48
  25.2 11.2 %collective-permute-start.6 = (bf16[48,2176]{1,0:T(8,128)(2,1)S(1)}, bf16[48,2176]{1,0:T(8,128)(2,1)S(1)}, u32[]{:S(2)}, u32[]{:S(2)}) collective-permute-start(bf16[48,2176]{1,0:T(8,128)(2,1)S(1)} %collective-permute-done.4.refs_0_.refs_5_), channel_id=1, source_target_pairs={{0,32},{32,64},{64,96},{96,128},{128,160},{160,192},{192,224},{224... | collective-permute-start | bytes 626696 | tf_op jit(solution)/shard_map/ppermute | solution.py:44
  25.6 1.0 copy-start.3
  26.6 7.0 %collective-permute-start.8 = (bf16[48,2048]{1,0:T(8,128)(2,1)S(1)}, bf16[48,2048]{1,0:T(8,128)(2,1)S(1)}, u32[]{:S(2)}, u32[]{:S(2)}) collective-permute-start(bf16[48,2048]{1,0:T(8,128)(2,1)S(1)} %narrow.1.refs_0_), channel_id=1, source_target_pairs={{0,224},{32,0},{64,32},{96,64},{128,96},{160,128},{192,160},{224,1... | collective-permute-start | bytes 589832 | tf_op jit(solution)/shard_map/ppermute | solution.py:48
  29.5 6.9 %collective-permute-start.7 = (bf16[48,2048]{1,0:T(8,128)(2,1)S(1)}, bf16[48,2048]{1,0:T(8,128)(2,1)S(1)}, u32[]{:S(2)}, u32[]{:S(2)}) collective-permute-start(bf16[48,2048]{1,0:T(8,128)(2,1)S(1)} %narrow.1.refs_0_), channel_id=1, source_target_pairs={{0,32},{32,64},{64,96},{96,128},{128,160},{160,192},{192,224},{224... | collective-permute-start | bytes 589832 | tf_op jit(solution)/shard_map/ppermute | solution.py:44
  36.4 0.9 copy-start.2
  39.8 35.0 %all-to-all-start = ((bf16[16,32,2048]{2,1,0:T(8,128)(2,1)}), bf16[16,32,2048]{2,1,0:T(8,128)(2,1)S(1)}, u32[]{:S(2)}, u32[]{:S(2)}) async-start(bf16[16,32,2048]{2,1,0:T(8,128)(2,1)} %bitcast.47), calls=%async_computation | async-start | bytes 4194304 | tf_op jit(solution)/shard_map/all_to_all | solution.py:354
  46.9 7.0 %collective-permute-start.9 = (bf16[48,2048]{1,0:T(8,128)(2,1)S(1)}, bf16[48,2048]{1,0:T(8,128)(2,1)S(1)}, u32[]{:S(2)}, u32[]{:S(2)}) collective-permute-start(bf16[48,2048]{1,0:T(8,128)(2,1)S(1)} %collective-permute-done.7.refs_8_.refs_1_), channel_id=1, source_target_pairs={{0,32},{32,64},{64,96},{96,128},{128,160},{160,192},{192,224},{224... | collective-permute-start | bytes 589832 | tf_op jit(solution)/shard_map/ppermute | solution.py:44
  47.4 32.6 %collective-permute-start.15 = (bf16[2048,384]{1,0:T(8,128)(2,1)}, bf16[2048,384]{1,0:T(8,128)(2,1)}, u32[]{:S(2)}, u32[]{:S(2)}) collective-permute-start(bf16[2048,384]{1,0:T(8,128)(2,1)} %bitcast.48), channel_id=1, source_target_pairs={{0,1},{1,0},{2,3},{3,2},{4,5},{5,4},{6,7},{7,6},{8,9},{9,8},{10,11... | collective-permute-start | bytes 4718600 | tf_op jit(solution)/shard_map/ppermute | solution.py:371
  47.4 8.8 %collective-permute-start.10 = (bf16[48,2048]{1,0:T(8,128)(2,1)S(1)}, bf16[48,2048]{1,0:T(8,128)(2,1)S(1)}, u32[]{:S(2)}, u32[]{:S(2)}) collective-permute-start(bf16[48,2048]{1,0:T(8,128)(2,1)S(1)} %collective-permute-done.8.refs_9_.refs_2_), channel_id=1, source_target_pairs={{0,224},{32,0},{64,32},{96,64},{128,96},{160,128},{192,160},{224,1... | collective-permute-start | bytes 589832 | tf_op jit(solution)/shard_map/ppermute | solution.py:48
  53.8 6.9 %collective-permute-start.11 = (bf16[48,2048]{1,0:T(8,128)(2,1)S(1)}, bf16[48,2048]{1,0:T(8,128)(2,1)S(1)}, u32[]{:S(2)}, u32[]{:S(2)}) collective-permute-start(bf16[48,2048]{1,0:T(8,128)(2,1)S(1)} %collective-permute-done.9.refs_3_), channel_id=1, source_target_pairs={{0,32},{32,64},{64,96},{96,128},{128,160},{160,192},{192,224},{224... | collective-permute-start | bytes 589832 | tf_op jit(solution)/shard_map/ppermute | solution.py:44
  53.8 28.4 %collective-permute-start.16 = (bf16[2048,384]{1,0:T(8,128)(2,1)}, bf16[2048,384]{1,0:T(8,128)(2,1)}, u32[]{:S(2)}, u32[]{:S(2)}) collective-permute-start(bf16[2048,384]{1,0:T(8,128)(2,1)} %bitcast.50), channel_id=1, source_target_pairs={{0,1},{1,0},{2,3},{3,2},{4,5},{5,4},{6,7},{7,6},{8,9},{9,8},{10,11... | collective-permute-start | bytes 4718600 | tf_op jit(solution)/shard_map/ppermute | solution.py:371
  56.2 8.2 %collective-permute-start.12 = (bf16[48,2048]{1,0:T(8,128)(2,1)S(1)}, bf16[48,2048]{1,0:T(8,128)(2,1)S(1)}, u32[]{:S(2)}, u32[]{:S(2)}) collective-permute-start(bf16[48,2048]{1,0:T(8,128)(2,1)S(1)} %collective-permute-done.10.refs_4_), channel_id=1, source_target_pairs={{0,224},{32,0},{64,32},{96,64},{128,96},{160,128},{192,160},{224,1... | collective-permute-start | bytes 589832 | tf_op jit(solution)/shard_map/ppermute | solution.py:48
  60.7 6.9 %collective-permute-start.13 = (bf16[48,2048]{1,0:T(8,128)(2,1)S(1)}, bf16[48,2048]{1,0:T(8,128)(2,1)S(1)}, u32[]{:S(2)}, u32[]{:S(2)}) collective-permute-start(bf16[48,2048]{1,0:T(8,128)(2,1)S(1)} %collective-permute-done.11.refs_5_), channel_id=1, source_target_pairs={{0,32},{32,64},{64,96},{96,128},{128,160},{160,192},{192,224},{224... | collective-permute-start | bytes 589832 | tf_op jit(solution)/shard_map/ppermute | solution.py:44
  74.8 1.3 copy-start.6
  76.1 33.3 %all-to-all-start.1 = ((bf16[16,32,2048]{2,1,0:T(8,128)(2,1)}), bf16[16,32,2048]{2,1,0:T(8,128)(2,1)S(1)}, u32[]{:S(2)}, u32[]{:S(2)}) async-start(bf16[16,32,2048]{2,1,0:T(8,128)(2,1)} %bitcast.41), calls=%async_computation.1 | async-start | bytes 4194304 | tf_op jit(solution)/shard_map/all_to_all | solution.py:354
  79.9 2.4 %copy-start.8 = (bf16[1,2048,384]{2,1,0:T(8,128)(2,1)S(1)}, bf16[1,2048,384]{2,1,0:T(8,128)(2,1)}, u32[]{:S(2)}) copy-start(bf16[1,2048,384]{2,1,0:T(8,128)(2,1)} %param.12) | copy-start | bytes 4718596
  79.9 5.2 %collective-permute-start.14 = (bf16[2048,384]{1,0:T(8,128)(2,1)}, bf16[2048,384]{1,0:T(8,128)(2,1)S(1)}, u32[]{:S(2)}, u32[]{:S(2)}) collective-permute-start(bf16[2048,384]{1,0:T(8,128)(2,1)} %bitcast.52), channel_id=1, source_target_pairs={{0,1},{1,0},{2,3},{3,2},{4,5},{5,4},{6,7},{7,6},{8,9},{9,8},{10,11... | collective-permute-start | bytes 4718600 | tf_op jit(solution)/shard_map/ppermute | solution.py:371
  82.2 5.3 %copy-start = (bf16[2048,768]{1,0:T(8,128)(2,1)}, bf16[2048,768]{1,0:T(8,128)(2,1)S(1)}, u32[]{:S(2)}) copy-start(bf16[2048,768]{1,0:T(8,128)(2,1)S(1)} %pad_maximum_fusion.1.wg_ref.wg_h) | copy-start | bytes 9437188
  82.2 3.0 %copy-start.9 = (bf16[1,2048,384]{2,1,0:T(8,128)(2,1)S(1)}, bf16[1,2048,384]{2,1,0:T(8,128)(2,1)}, u32[]{:S(2)}) copy-start(bf16[1,2048,384]{2,1,0:T(8,128)(2,1)} %param.13) | copy-start | bytes 4718596
  85.1 2.7 %copy-start.1 = (bf16[2048,768]{1,0:T(8,128)(2,1)}, bf16[2048,768]{1,0:T(8,128)(2,1)S(1)}, u32[]{:S(2)}) copy-start(bf16[2048,768]{1,0:T(8,128)(2,1)S(1)} %pad_maximum_fusion.2.wu_ref.wu_h) | copy-start | bytes 9437188
  109.5 1.4 copy-start.4
  122.2 10.0 %copy-start.12 = (bf16[512,768]{1,0:T(8,128)(2,1)S(1)}, bf16[512,768]{1,0:T(8,128)(2,1)}, u32[]{:S(2)}) copy-start(bf16[512,768]{1,0:T(8,128)(2,1)} %get-tuple-element.23) | copy-start | bytes 2359300
  122.2 64.0 %all-to-all-start.2 = ((bf16[128,4,2048]{2,1,0:T(4,128)(2,1)}), bf16[128,4,2048]{2,1,0:T(4,128)(2,1)S(1)}, u32[]{:S(2)}, u32[]{:S(2)}) async-start(bf16[128,4,2048]{2,1,0:T(4,128)(2,1)} %get-tuple-element.20), calls=%async_computation.2 | async-start | bytes 4194304 | tf_op jit(solution)/shard_map/all_to_all | solution.py:377
  132.2 3.2 %copy-start.7 = (bf16[16,32,2048]{2,1,0:T(8,128)(2,1)S(1)}, bf16[16,32,2048]{2,1,0:T(8,128)(2,1)}, u32[]{:S(2)}) copy-start(bf16[16,32,2048]{2,1,0:T(8,128)(2,1)} %copy-done.6) | copy-start | bytes 6291460
  132.2 3.2 %copy-start.13 = (bf16[512,768]{1,0:T(8,128)(2,1)S(1)}, bf16[512,768]{1,0:T(8,128)(2,1)}, u32[]{:S(2)}) copy-start(bf16[512,768]{1,0:T(8,128)(2,1)} %get-tuple-element.22) | copy-start | bytes 2359300
  135.2 3.9 %collective-permute-start.19 = (bf16[2048,384]{1,0:T(8,128)(2,1)S(1)}, bf16[2048,384]{1,0:T(8,128)(2,1)S(1)}, u32[]{:S(2)}, u32[]{:S(2)}) collective-permute-start(bf16[2048,384]{1,0:T(8,128)(2,1)S(1)} %convolution_convert_fusion), channel_id=1, source_target_pairs={{0,1},{1,0},{2,3},{3,2},{4,5},{5,4},{6,7},{7,6},{8,9},{9,8},{10,11... | collective-permute-start | bytes 4718600 | tf_op jit(solution)/shard_map/ppermute | solution.py:382
  135.4 1.9 %copy-start.11 = (bf16[512,768]{1,0:T(8,128)(2,1)S(1)}, bf16[512,768]{1,0:T(8,128)(2,1)}, u32[]{:S(2)}) copy-start(bf16[512,768]{1,0:T(8,128)(2,1)} %get-tuple-element.21) | copy-start | bytes 2359300
  136.7 6.0 %collective-permute-start.18 = (bf16[2048,384]{1,0:T(8,128)(2,1)S(1)}, bf16[2048,384]{1,0:T(8,128)(2,1)S(1)}, u32[]{:S(2)}, u32[]{:S(2)}) collective-permute-start(bf16[2048,384]{1,0:T(8,128)(2,1)S(1)} %convolution_convert_fusion.2), channel_id=1, source_target_pairs={{0,1},{1,0},{2,3},{3,2},{4,5},{5,4},{6,7},{7,6},{8,9},{9,8},{10,11... | collective-permute-start | bytes 4718600 | tf_op jit(solution)/shard_map/ppermute | solution.py:382
  137.2 1.5 copy-start.10
  138.6 1.6 copy-start.5
  138.6 6.6 %collective-permute-start.17 = (bf16[2048,384]{1,0:T(8,128)(2,1)S(1)}, bf16[2048,384]{1,0:T(8,128)(2,1)S(1)}, u32[]{:S(2)}, u32[]{:S(2)}) collective-permute-start(bf16[2048,384]{1,0:T(8,128)(2,1)S(1)} %convolution_convert_fusion.4), channel_id=1, source_target_pairs={{0,1},{1,0},{2,3},{3,2},{4,5},{5,4},{6,7},{7,6},{8,9},{9,8},{10,11... | collective-permute-start | bytes 4718600 | tf_op jit(solution)/shard_map/ppermute | solution.py:382
where the time goes:
time: 188 us; the launch traced here: 187 us
  waiting for transfers between devices  93.8 us (50%)
  starting transfers between devices  39.5 us (21%)
  Pallas kernels  26.4 us (14%)
  matrix products  13.5 us (7%)
  other arithmetic  7.33 us (4%)
  local copies, waits for them, and re-layouts  6.1 us (3%)
    all_to_all x1, waiting for transfers between devices, per_device(): lax.all_to_all(dxs, ('y', 'x', 'z'), split_axis=0, concat_axis=0, tiled=T...  38.5 us
    ppermute x8, waiting for transfers between devices, along_z(): below = lax.ppermute(below, 'z', up)  25.4 us
    all_to_all x2, waiting for transfers between devices, in_plane(): lax.all_to_all(rows.reshape(PLANE, block, width), ('y', 'x'), split_axis=...  19.5 us
    dot_general x7, matrix products, mm(): lax.dot_general(a, b, ((dims[0], dims[1]), ((), ())), preferred_element_t...  13.5 us
    ppermute x6, starting transfers between devices, along_z(): above = lax.ppermute(above, 'z', down)  13 us
    pallas_call x1, Pallas kernels, backward(): pl.pallas_call(body, in_specs=[IN_HBM] * 6, out_specs=[IN_HBM] * 3, out_s...  11.3 us
    all_to_all x2, starting transfers between devices, in_plane(): lax.all_to_all(rows.reshape(PLANE, block, width), ('y', 'x'), split_axis=...  10.8 us
    ppermute x6, waiting for transfers between devices, along_z(): above = lax.ppermute(above, 'z', down)  10.4 us
  transfers between devices with their start and end apart: 23, of which 15 were waited for; matrix products, arithmetic and copies ran while one was open for 11% of the time, Pallas kernels for 5%

commit v1 on v0

--- a/solution.py
+++ b/solution.py
@@ -35,20 +35,16 @@
     return named, prob
 
 
-def along_z(rows, depth):
-    up = [(i, (i + 1) % depth) for i in range(depth)]
-    down = [(i, (i - 1) % depth) for i in range(depth)]
-    below = above = rows
-    blocks, offsets = [rows], [0]
+def along_z(rows, depth, first):
+    found = {0: rows}
+    ahead = behind = rows
     for step in range(1, depth // 2 + 1):
-        below = lax.ppermute(below, "z", up)
-        blocks.append(below)
-        offsets.append(depth - step)
+        ahead = lax.ppermute(ahead, "z", [(i, (i + first) % depth) for i in range(depth)])
+        found[-first * step % depth] = ahead
         if step < depth - step:
-            above = lax.ppermute(above, "z", down)
-            blocks.append(above)
-            offsets.append(step)
-    return blocks, offsets
+            behind = lax.ppermute(behind, "z", [(i, (i - first) % depth) for i in range(depth)])
+            found[first * step % depth] = behind
+    return found
 
 
 def iota(shape, dim):
@@ -187,10 +183,7 @@
     rows, width = xs.shape
     hidden = wg.shape[1]
 
-    def body(x_h, wg_ref, wu_ref, act_h, slope_h, hid_h, act_ref, slope_ref, hid_ref, x_ref, sems):
-        arrive = pltpu.make_async_copy(x_h, x_ref, sems.at[3])
-        arrive.start()
-        arrive.wait()
+    def body(x_ref, wg_ref, wu_ref, act_h, slope_h, hid_h, act_ref, slope_ref, hid_ref, sems):
         for i in range(0, hidden, part):
             a = mm(x_ref[...], wg_ref[:, i : i + part], ((1,), (0,)))
             b = mm(x_ref[...], wu_ref[:, i : i + part], ((1,), (0,)))
@@ -210,7 +203,7 @@
 
     return pl.pallas_call(
         body,
-        in_specs=[IN_HBM, IN_VMEM, IN_VMEM],
+        in_specs=[IN_VMEM] * 3,
         out_specs=[IN_HBM] * 3,
         out_shape=[
             pltpu.HBM((rows, hidden), F32),
@@ -221,12 +214,11 @@
             pltpu.VMEM((rows, hidden), F32),
             pltpu.VMEM((rows, hidden), F32),
             pltpu.VMEM((rows, hidden), BF16),
-            pltpu.VMEM((rows, width), BF16),
-            pltpu.SemaphoreType.DMA((4,)),
+            pltpu.SemaphoreType.DMA((3,)),
         ],
         compiler_params=pltpu.CompilerParams(vmem_limit_bytes=2 * SCOPED),
         name="activations",
-    )(pltpu.with_memory_space_constraint(xs, pltpu.HBM), wg, wu)
+    )(pltpu.with_memory_space_constraint(xs, pltpu.VMEM), wg, wu)
 
 
 def combine(pick, rows, parts):
@@ -292,6 +284,8 @@
             dh = mm(go_ref[...], wd_ref[:, i : i + part], ((1,), (0,)))
             da_ref[:, i : i + part] = (dh * slope_ref[:, i : i + part]).astype(BF16)
             db_ref[:, i : i + part] = (dh * act_ref[:, i : i + part]).astype(BF16)
+        for copy in keep:
+            copy.start()
         for copy in later:
             copy.wait()
         for i in range(0, width, chunk):
@@ -300,8 +294,6 @@
             )
             dxs_ref[:, :, i : i + chunk] = dxs.reshape(shape[0], cap, chunk).astype(BF16)
             send(i).start()
-        for copy in keep:
-            copy.start()
         for i in range(0, width, chunk):
             send(i).wait()
         for copy in keep:
@@ -343,11 +335,15 @@
     total_slots = peers * slot_cap
     swap = [(0, 1), (1, 0)]
 
-    column, came_from = along_z(prepare(hidden_in, route_ids.T, route_prob.T), depth)
-    g_column, _ = along_z(narrow(out_grad, column[-3:-1]), depth)
+    x_at = along_z(prepare(hidden_in, route_ids.T, route_prob.T), depth, 1)
+    last = depth // 2
+    g_at = along_z(narrow(out_grad, [x_at[depth + 1 - last]]), depth, -1)
+    came_from = sorted(x_at)
+    column = [x_at[offset] for offset in came_from]
+    g_column = [g_at[offset] for offset in came_from]
     block = depth * slot_cap
     send_x, weigh = fill_x(
-        column, came_from, lax.axis_index("z").reshape(1), top_count, slot_cap, width, 4, g_column[1:3]
+        column, came_from, lax.axis_index("z").reshape(1), top_count, slot_cap, width, 4, [g_at[1]]
     )
 
     def in_plane(rows):

time: 188 us -> 176 us (0.936)
  waiting for transfers between devices: 93.8 us -> 79 us
  starting transfers between devices: 39.5 us -> 44.4 us
  Pallas kernels: 26.4 us -> 24.3 us
    all_to_all x2, waiting for transfers between devices: 19.5 us -> 14.1 us  [in_plane(): lax.all_to_all(rows.reshape(PLANE, block, width), ('y', 'x'), split_axis=...]
    ppermute x14, waiting for transfers between devices: 35.8 us -> 30.9 us  [the longest x8 21.3 us: along_z(): lax.ppermute(ahead, 'z', [(i, (i + first) % depth) for i in range(depth)])]
    all_to_all x1, waiting for transfers between devices: 38.5 us -> 34 us  [per_device(): lax.all_to_all(dxs, ('y', 'x', 'z'), split_axis=0, concat_axis=0, tiled=T...]
    ppermute x14, starting transfers between devices: 17.8 us -> 22.2 us  [the longest x6 15 us: along_z(): lax.ppermute(behind, 'z', [(i, (i - first) % depth) for i in range(depth)])]
    all_to_all x2, starting transfers between devices: 10.8 us -> 12.9 us  [in_plane(): lax.all_to_all(rows.reshape(PLANE, block, width), ('y', 'x'), split_axis=...]
    unnamed x28 -> x26, local copies, waits for them, and re-layouts: 6.09 us -> 4.56 us
  transfers between devices with their start and end apart: 23 -> 23, of which waited for: 15 -> 14; matrix products, arithmetic and copies ran while one was open for 11% -> 13% of each run, Pallas kernels for 5% -> 4%
where the time goes in v1:
time: 176 us; the launch traced here: 175 us
  waiting for transfers between devices  79 us (45%)
  starting transfers between devices  44.4 us (25%)
  Pallas kernels  24.3 us (14%)
  matrix products  15.1 us (9%)
  other arithmetic  7.01 us (4%)
  local copies, waits for them, and re-layouts  4.57 us (3%)
    all_to_all x1, waiting for transfers between devices, per_device(): lax.all_to_all(dxs, ('y', 'x', 'z'), split_axis=0, concat_axis=0, tiled=T...  34 us
    ppermute x8, waiting for transfers between devices, along_z(): lax.ppermute(ahead, 'z', [(i, (i + first) % depth) for i in range(depth)])  21.3 us
    dot_general x7, matrix products, mm(): lax.dot_general(a, b, ((dims[0], dims[1]), ((), ())), preferred_element_t...  15.1 us
    ppermute x6, starting transfers between devices, along_z(): lax.ppermute(behind, 'z', [(i, (i - first) % depth) for i in range(depth)])  15 us
    all_to_all x2, waiting for transfers between devices, in_plane(): lax.all_to_all(rows.reshape(PLANE, block, width), ('y', 'x'), split_axis=...  14.1 us
    all_to_all x2, starting transfers between devices, in_plane(): lax.all_to_all(rows.reshape(PLANE, block, width), ('y', 'x'), split_axis=...  12.9 us
    pallas_call x1, Pallas kernels, backward(): pl.pallas_call(body, in_specs=[IN_HBM] * 6, out_specs=[IN_HBM] * 3, out_s...  10.8 us
    ppermute x6, waiting for transfers between devices, along_z(): lax.ppermute(behind, 'z', [(i, (i - first) % depth) for i in range(depth)])  9.63 us
  transfers between devices with their start and end apart: 23, of which 14 were waited for; matrix products, arithmetic and copies ran while one was open for 13% of the time, Pallas kernels for 4%

profile of v1, /device:TPU:32, one launch (start us, length us, event | category | flops | bytes accessed | tf_op | source)
XLA Modules:
  0.0 175.3 jit_solution(5485991593976643602)
XLA Ops:
  0.6 1.9 %prepare.1.refs_0_ = bf16[48,2176]{1,0:T(8,128)(2,1)} custom-call(f32[48,2048]{1,0:T(8,128)} %x_ref.2, s32[8,48]{1,0:T(8,128)} %bitcast.51, f32[8,48]{1,0:T(8,128)} %bitcast.53), custom_call_target="tpu_custom_call" | custom-call | tf_op jit(solution)/shard_map/prepare/pallas_call | solution.py:64
  2.5 1.9 %collective-permute-start.3 = (bf16[48,2176]{1,0:T(8,128)(2,1)}, bf16[48,2176]{1,0:T(8,128)(2,1)S(1)}, u32[]{:S(2)}, u32[]{:S(2)}) collective-permute-start(bf16[48,2176]{1,0:T(8,128)(2,1)} %prepare.1.refs_0_), channel_id=1, source_target_pairs={{0,32},{32,64},{64,96},{96,128},{128,160},{160,192},{192,224},{224... | collective-permute-start | bytes 626696 | tf_op jit(solution)/shard_map/ppermute | solution.py:42
  4.5 5.1 %collective-permute-done.3.refs_7_ = bf16[48,2176]{1,0:T(8,128)(2,1)S(1)} collective-permute-done((bf16[48,2176]{1,0:T(8,128)(2,1)}, bf16[48,2176]{1,0:T(8,128)(2,1)S(1)}, u32[]{:S(2)}, u32[]{:S(2)}) %collective-permute-start.3) | collective-permute-done | bytes 208928 | tf_op jit(solution)/shard_map/ppermute | solution.py:42
  9.6 1.9 %collective-permute-start.4 = (bf16[48,2176]{1,0:T(8,128)(2,1)S(1)}, bf16[48,2176]{1,0:T(8,128)(2,1)S(1)}, u32[]{:S(2)}, u32[]{:S(2)}) collective-permute-start(bf16[48,2176]{1,0:T(8,128)(2,1)S(1)} %collective-permute-done.3.refs_7_), channel_id=1, source_target_pairs={{0,32},{32,64},{64,96},{96,128},{128,160},{160,192},{192,224},{224... | collective-permute-start | bytes 626696 | tf_op jit(solution)/shard_map/ppermute | solution.py:42
  11.5 2.3 %collective-permute-start.1 = (bf16[48,2176]{1,0:T(8,128)(2,1)S(1)}, bf16[48,2176]{1,0:T(8,128)(2,1)S(1)}, u32[]{:S(2)}, u32[]{:S(2)}) collective-permute-start(bf16[48,2176]{1,0:T(8,128)(2,1)S(1)} %collective-permute-done.refs_1_), channel_id=1, source_target_pairs={{0,224},{32,0},{64,32},{96,64},{128,96},{160,128},{192,160},{224,1... | collective-permute-start | bytes 626696 | tf_op jit(solution)/shard_map/ppermute | solution.py:45
  13.9 4.6 %collective-permute-done.4.refs_6_ = bf16[48,2176]{1,0:T(8,128)(2,1)S(1)} collective-permute-done((bf16[48,2176]{1,0:T(8,128)(2,1)S(1)}, bf16[48,2176]{1,0:T(8,128)(2,1)S(1)}, u32[]{:S(2)}, u32[]{:S(2)}) %collective-permute-start.4) | collective-permute-done | bytes 208928 | tf_op jit(solution)/shard_map/ppermute | solution.py:42
  18.5 0.4 collective-permute-done.1.refs_2_
  18.9 2.5 %collective-permute-start.2 = (bf16[48,2176]{1,0:T(8,128)(2,1)S(1)}, bf16[48,2176]{1,0:T(8,128)(2,1)S(1)}, u32[]{:S(2)}, u32[]{:S(2)}) collective-permute-start(bf16[48,2176]{1,0:T(8,128)(2,1)S(1)} %collective-permute-done.1.refs_2_), channel_id=1, source_target_pairs={{0,224},{32,0},{64,32},{96,64},{128,96},{160,128},{192,160},{224,1... | collective-permute-start | bytes 626696 | tf_op jit(solution)/shard_map/ppermute | solution.py:45
  21.4 3.8 %collective-permute-done.5.refs_0_.refs_5_ = bf16[48,2176]{1,0:T(8,128)(2,1)S(1)} collective-permute-done((bf16[48,2176]{1,0:T(8,128)(2,1)S(1)}, bf16[48,2176]{1,0:T(8,128)(2,1)S(1)}, u32[]{:S(2)}, u32[]{:S(2)}) %collective-permute-start.5) | collective-permute-done | bytes 208928 | tf_op jit(solution)/shard_map/ppermute | solution.py:42
  25.2 1.0 copy-done.6
  26.2 3.3 %collective-permute-start.7 = (bf16[48,2048]{1,0:T(8,128)(2,1)S(1)}, bf16[48,2048]{1,0:T(8,128)(2,1)S(1)}, u32[]{:S(2)}, u32[]{:S(2)}) collective-permute-start(bf16[48,2048]{1,0:T(8,128)(2,1)S(1)} %narrow.1.refs_0_), channel_id=1, source_target_pairs={{0,224},{32,0},{64,32},{96,64},{128,96},{160,128},{192,160},{224,1... | collective-permute-start | bytes 589832 | tf_op jit(solution)/shard_map/ppermute | solution.py:42
  29.5 3.6 %collective-permute-done.7.refs_8_.refs_1_ = bf16[48,2048]{1,0:T(8,128)(2,1)S(1)} collective-permute-done((bf16[48,2048]{1,0:T(8,128)(2,1)S(1)}, bf16[48,2048]{1,0:T(8,128)(2,1)S(1)}, u32[]{:S(2)}, u32[]{:S(2)}) %collective-permute-start.7) | collective-permute-done | bytes 196640 | tf_op jit(solution)/shard_map/ppermute | solution.py:42
  33.1 0.9 copy-done.5
  34.0 2.5 %fill_x.1 = (bf16[512,2048]{1,0:T(8,128)(2,1)}, bf16[512,384]{1,0:T(8,128)(2,1)S(1)}) custom-call(s32[1]{0:T(128)} %bitcast.9.z_ref, bf16[48,2176]{1,0:T(8,128)(2,1)S(1)} %copy-done.5, bf16[48,2176]{1,0:T(8,128)(2,1)S(1)} %collective-permute-done.refs_1_, bf16[48,2176]{1,0:T(8,128)(2,1)S(1)} %collective-permute-done.1.refs_2_, ...), custom_call_target="tpu_custom_call" | custom-call | tf_op jit(solution)/shard_map/fill_x/pallas_call | solution.py:137
  36.5 7.0 %all-to-all-start = ((bf16[16,32,2048]{2,1,0:T(8,128)(2,1)}), bf16[16,32,2048]{2,1,0:T(8,128)(2,1)S(1)}, u32[]{:S(2)}, u32[]{:S(2)}) async-start(bf16[16,32,2048]{2,1,0:T(8,128)(2,1)} %bitcast.44), calls=%async_computation | async-start | bytes 4194304 | tf_op jit(solution)/shard_map/all_to_all | solution.py:350
  43.6 3.8 %collective-permute-start.11 = (bf16[48,2048]{1,0:T(8,128)(2,1)S(1)}, bf16[48,2048]{1,0:T(8,128)(2,1)S(1)}, u32[]{:S(2)}, u32[]{:S(2)}) collective-permute-start(bf16[48,2048]{1,0:T(8,128)(2,1)S(1)} %narrow.1.refs_0_), channel_id=1, source_target_pairs={{0,32},{32,64},{64,96},{96,128},{128,160},{160,192},{192,224},{224... | collective-permute-start | bytes 589832 | tf_op jit(solution)/shard_map/ppermute | solution.py:45
  47.4 3.2 %collective-permute-done.11.refs_7_ = bf16[48,2048]{1,0:T(8,128)(2,1)S(1)} collective-permute-done((bf16[48,2048]{1,0:T(8,128)(2,1)S(1)}, bf16[48,2048]{1,0:T(8,128)(2,1)S(1)}, u32[]{:S(2)}, u32[]{:S(2)}) %collective-permute-start.11) | collective-permute-done | bytes 196640 | tf_op jit(solution)/shard_map/ppermute | solution.py:45
  50.6 3.7 %collective-permute-start.12 = (bf16[48,2048]{1,0:T(8,128)(2,1)S(1)}, bf16[48,2048]{1,0:T(8,128)(2,1)S(1)}, u32[]{:S(2)}, u32[]{:S(2)}) collective-permute-start(bf16[48,2048]{1,0:T(8,128)(2,1)S(1)} %collective-permute-done.11.refs_7_), channel_id=1, source_target_pairs={{0,32},{32,64},{64,96},{96,128},{128,160},{160,192},{192,224},{224... | collective-permute-start | bytes 589832 | tf_op jit(solution)/shard_map/ppermute | solution.py:45
  54.3 0.5 collective-permute-done.8.refs_2_
  54.7 2.8 %collective-permute-done.12.refs_6_ = bf16[48,2048]{1,0:T(8,128)(2,1)S(1)} collective-permute-done((bf16[48,2048]{1,0:T(8,128)(2,1)S(1)}, bf16[48,2048]{1,0:T(8,128)(2,1)S(1)}, u32[]{:S(2)}, u32[]{:S(2)}) %collective-permute-start.12) | collective-permute-done | bytes 196640 | tf_op jit(solution)/shard_map/ppermute | solution.py:45
  57.5 2.6 %collective-permute-start.13 = (bf16[48,2048]{1,0:T(8,128)(2,1)S(1)}, bf16[48,2048]{1,0:T(8,128)(2,1)S(1)}, u32[]{:S(2)}, u32[]{:S(2)}) collective-permute-start(bf16[48,2048]{1,0:T(8,128)(2,1)S(1)} %collective-permute-done.12.refs_6_), channel_id=1, source_target_pairs={{0,32},{32,64},{64,96},{96,128},{128,160},{160,192},{192,224},{224... | collective-permute-start | bytes 589832 | tf_op jit(solution)/shard_map/ppermute | solution.py:45
  60.1 1.1 collective-permute-done.9.refs_3_
  61.1 3.2 %collective-permute-done.13.refs_5_ = bf16[48,2048]{1,0:T(8,128)(2,1)S(1)} collective-permute-done((bf16[48,2048]{1,0:T(8,128)(2,1)S(1)}, bf16[48,2048]{1,0:T(8,128)(2,1)S(1)}, u32[]{:S(2)}, u32[]{:S(2)}) %collective-permute-start.13) | collective-permute-done | bytes 196640 | tf_op jit(solution)/shard_map/ppermute | solution.py:45
  64.4 2.7 %collective-permute-done.10.refs_4_ = bf16[48,2048]{1,0:T(8,128)(2,1)S(1)} collective-permute-done((bf16[48,2048]{1,0:T(8,128)(2,1)S(1)}, bf16[48,2048]{1,0:T(8,128)(2,1)S(1)}, u32[]{:S(2)}, u32[]{:S(2)}) %collective-permute-start.10) | collective-permute-done | bytes 196640 | tf_op jit(solution)/shard_map/ppermute | solution.py:42
  67.1 2.2 %fill_g.1 = bf16[512,2048]{1,0:T(8,128)(2,1)} custom-call(bf16[512,384]{1,0:T(8,128)(2,1)S(1)} %get-tuple-element.14.weigh_ref, bf16[48,2048]{1,0:T(8,128)(2,1)S(1)} %narrow.1.refs_0_, bf16[48,2048]{1,0:T(8,128)(2,1)S(1)} %collective-permute-done.7.refs_8_.refs_1_, bf16[48,2048]{1,0:T(8,128)(2,1)S(1)} %collective-permute-done.8.refs_2_, ...), custom_call_target="tpu_custom_call" | custom-call | tf_op jit(solution)/shard_map/fill_g/pallas_call | solution.py:171
  69.3 1.3 all-to-all-done
  70.6 1.4 copy-done.2
  72.0 5.9 %all-to-all-start.1 = ((bf16[16,32,2048]{2,1,0:T(8,128)(2,1)}), bf16[16,32,2048]{2,1,0:T(8,128)(2,1)}, u32[]{:S(2)}, u32[]{:S(2)}) async-start(bf16[16,32,2048]{2,1,0:T(8,128)(2,1)} %bitcast.43), calls=%async_computation.1 | async-start | bytes 4194304 | tf_op jit(solution)/shard_map/all_to_all | solution.py:350
  78.0 2.2 %pad_maximum_fusion.1.wg_ref.wg_h = bf16[2048,768]{1,0:T(8,128)(2,1)S(1)} fusion(bf16[2048,384]{1,0:T(8,128)(2,1)} %collective-permute-done.15, bf16[2048,384]{1,0:T(8,128)(2,1)} %bitcast.46), kind=kLoop, calls=%fused_computation.1 | loop fusion | flops 6291456 | bytes 6291456 | tf_op jit(solution)/shard_map/concatenate | solution.py:367
  80.3 2.8 %pad_maximum_fusion.2.wu_ref.wu_h = bf16[2048,768]{1,0:T(8,128)(2,1)S(1)} fusion(bf16[2048,384]{1,0:T(8,128)(2,1)} %collective-permute-done.16, bf16[2048,384]{1,0:T(8,128)(2,1)S(1)} %bitcast.48), kind=kLoop, calls=%fused_computation.2 | loop fusion | flops 6291456 | bytes 6291456 | tf_op jit(solution)/shard_map/concatenate | solution.py:367
  83.1 0.1 copy-done.8
  83.2 1.9 %pad_maximum_fusion.wd_h = bf16[2048,768]{1,0:T(8,128)(2,1)} fusion(bf16[2048,384]{1,0:T(8,128)(2,1)S(1)} %collective-permute-done.14, bf16[2048,384]{1,0:T(8,128)(2,1)S(1)} %bitcast.50), kind=kLoop, calls=%fused_computation | loop fusion | flops 6291456 | bytes 6291456 | tf_op jit(solution)/shard_map/concatenate | solution.py:367
  85.2 0.7 copy-done.1
  85.9 0.3 copy-done.3
  86.3 5.6 %activations.1 = (f32[512,768]{1,0:T(8,128)}, f32[512,768]{1,0:T(8,128)}, bf16[512,768]{1,0:T(8,128)(2,1)}) custom-call(bf16[512,2048]{1,0:T(8,128)(2,1)S(1)} %bitcast.38, bf16[2048,768]{1,0:T(8,128)(2,1)S(1)} %pad_maximum_fusion.1.wg_ref.wg_h, bf16[2048,768]{1,0:T(8,128)(2,1)S(1)} %pad_maximum_fusion.2.wu_ref.wu_h), custom_call_target="tpu_custom_call" | custom-call | tf_op jit(solution)/shard_map/activations/pallas_call | solution.py:204
  91.9 12.8 %all-to-all-done.1 = bf16[16,32,2048]{2,1,0:T(8,128)(2,1)} async-done(((bf16[16,32,2048]{2,1,0:T(8,128)(2,1)}), bf16[16,32,2048]{2,1,0:T(8,128)(2,1)}, u32[]{:S(2)}, u32[]{:S(2)}) %all-to-all-start.1) | async-done | bytes 2097184 | tf_op jit(solution)/shard_map/all_to_all | solution.py:350
  104.7 10.8 %backward.1 = (bf16[128,4,2048]{2,1,0:T(4,128)(2,1)}, bf16[512,768]{1,0:T(8,128)(2,1)}, bf16[512,768]{1,0:T(8,128)(2,1)}) custom-call(bf16[512,2048]{1,0:T(8,128)(2,1)} %bitcast.14.go_h, bf16[2048,768]{1,0:T(8,128)(2,1)} %pad_maximum_fusion.wd_h, f32[512,768]{1,0:T(8,128)} %get-tuple-element.18.act_h, f32[512,768]{1,0:T(8,128)} %get-tuple-element.19.slope_h, ...), custom_call_target="tpu_custom_call" | custom-call | tf_op jit(solution)/shard_map/backward/pallas_call | solution.py:302
  115.5 8.5 %all-to-all-start.2 = ((bf16[128,4,2048]{2,1,0:T(4,128)(2,1)}), bf16[128,4,2048]{2,1,0:T(4,128)(2,1)S(1)}, u32[]{:S(2)}, u32[]{:S(2)}) async-start(bf16[128,4,2048]{2,1,0:T(4,128)(2,1)} %get-tuple-element.20), calls=%async_computation.2 | async-start | bytes 4194304 | tf_op jit(solution)/shard_map/all_to_all | solution.py:373
  124.0 3.0 %convolution_convert_fusion = bf16[2048,384]{1,0:T(8,128)(2,1)S(1)} fusion(bf16[512,2048]{1,0:T(8,128)(2,1)} %bitcast.14.go_h, bf16[512,768]{1,0:T(8,128)(2,1)S(1)} %copy-done.11), kind=kOutput, calls=%fused_computation.6 | convolution fusion | flops 806092800 | bytes 4063232 | tf_op jit(solution)/shard_map/dot_general | solution.py:18
  127.2 1.3 convolution_convert_fusion.2
  128.5 0.6 collective-permute-start.18
  129.1 1.3 convolution_convert_fusion.4
  130.6 0.4 fusion.4.pick_ref
  131.0 4.1 %fusion.2 = bf16[1,2048,384]{2,1,0:T(8,128)(2,1)} fusion(bf16[2048,384]{1,0:T(8,128)(2,1)S(1)} %collective-permute-done.19, bf16[512,2048]{1,0:T(8,128)(2,1)} %bitcast.14.go_h, bf16[512,768]{1,0:T(8,128)(2,1)S(1)} %copy-done.11), kind=kOutput, calls=%fused_computation.14 | convolution fusion | flops 809238528 | bytes 5636096 | tf_op jit(solution)/shard_map/dot_general | solution.py:18
  135.1 2.5 %fusion.1 = bf16[1,2048,384]{2,1,0:T(8,128)(2,1)} fusion(bf16[2048,384]{1,0:T(8,128)(2,1)S(1)} %collective-permute-done.18, bf16[512,2048]{1,0:T(8,128)(2,1)S(1)} %bitcast.41, bf16[512,768]{1,0:T(8,128)(2,1)S(1)} %copy-done.12), kind=kOutput, calls=%fused_computation.13 | convolution fusion | flops 809238528 | bytes 5636096 | tf_op jit(solution)/shard_map/dot_general | solution.py:18
  137.5 2.5 %fusion = bf16[1,2048,384]{2,1,0:T(8,128)(2,1)} fusion(bf16[2048,384]{1,0:T(8,128)(2,1)S(1)} %collective-permute-done.17, bf16[512,2048]{1,0:T(8,128)(2,1)S(1)} %bitcast.42, bf16[512,768]{1,0:T(8,128)(2,1)S(1)} %copy-done.10), kind=kOutput, calls=%fused_computation.12 | convolution fusion | flops 809238528 | bytes 5636096 | tf_op jit(solution)/shard_map/dot_general | solution.py:18
  140.0 34.0 %all-to-all-done.2.rows_ref = bf16[128,4,2048]{2,1,0:T(4,128)(2,1)S(1)} async-done(((bf16[128,4,2048]{2,1,0:T(4,128)(2,1)}), bf16[128,4,2048]{2,1,0:T(4,128)(2,1)S(1)}, u32[]{:S(2)}, u32[]{:S(2)}) %all-to-all-start.2) | async-done | bytes 2097184 | tf_op jit(solution)/shard_map/all_to_all | solution.py:373
  174.0 1.3 combine.1
  (45 shorter events, 0.6 us)
Async XLA Ops:
  2.5 7.1 %collective-permute-start.3 = (bf16[48,2176]{1,0:T(8,128)(2,1)}, bf16[48,2176]{1,0:T(8,128)(2,1)S(1)}, u32[]{:S(2)}, u32[]{:S(2)}) collective-permute-start(bf16[48,2176]{1,0:T(8,128)(2,1)} %prepare.1.refs_0_), channel_id=1, source_target_pairs={{0,32},{32,64},{64,96},{96,128},{128,160},{160,192},{192,224},{224... | collective-permute-start | bytes 626696 | tf_op jit(solution)/shard_map/ppermute | solution.py:42
  4.4 7.1 %collective-permute-start = (bf16[48,2176]{1,0:T(8,128)(2,1)}, bf16[48,2176]{1,0:T(8,128)(2,1)S(1)}, u32[]{:S(2)}, u32[]{:S(2)}) collective-permute-start(bf16[48,2176]{1,0:T(8,128)(2,1)} %prepare.1.refs_0_), channel_id=1, source_target_pairs={{0,224},{32,0},{64,32},{96,64},{128,96},{160,128},{192,160},{224,1... | collective-permute-start | bytes 626696 | tf_op jit(solution)/shard_map/ppermute | solution.py:45
  9.6 8.8 %collective-permute-start.4 = (bf16[48,2176]{1,0:T(8,128)(2,1)S(1)}, bf16[48,2176]{1,0:T(8,128)(2,1)S(1)}, u32[]{:S(2)}, u32[]{:S(2)}) collective-permute-start(bf16[48,2176]{1,0:T(8,128)(2,1)S(1)} %collective-permute-done.3.refs_7_), channel_id=1, source_target_pairs={{0,32},{32,64},{64,96},{96,128},{128,160},{160,192},{192,224},{224... | collective-permute-start | bytes 626696 | tf_op jit(solution)/shard_map/ppermute | solution.py:42
  11.5 7.3 %collective-permute-start.1 = (bf16[48,2176]{1,0:T(8,128)(2,1)S(1)}, bf16[48,2176]{1,0:T(8,128)(2,1)S(1)}, u32[]{:S(2)}, u32[]{:S(2)}) collective-permute-start(bf16[48,2176]{1,0:T(8,128)(2,1)S(1)} %collective-permute-done.refs_1_), channel_id=1, source_target_pairs={{0,224},{32,0},{64,32},{96,64},{128,96},{160,128},{192,160},{224,1... | collective-permute-start | bytes 626696 | tf_op jit(solution)/shard_map/ppermute | solution.py:45
  18.5 6.7 %collective-permute-start.5 = (bf16[48,2176]{1,0:T(8,128)(2,1)S(1)}, bf16[48,2176]{1,0:T(8,128)(2,1)S(1)}, u32[]{:S(2)}, u32[]{:S(2)}) collective-permute-start(bf16[48,2176]{1,0:T(8,128)(2,1)S(1)} %collective-permute-done.4.refs_6_), channel_id=1, source_target_pairs={{0,32},{32,64},{64,96},{96,128},{128,160},{160,192},{192,224},{224... | collective-permute-start | bytes 626696 | tf_op jit(solution)/shard_map/ppermute | solution.py:42
  18.9 10.6 %collective-permute-start.2 = (bf16[48,2176]{1,0:T(8,128)(2,1)S(1)}, bf16[48,2176]{1,0:T(8,128)(2,1)S(1)}, u32[]{:S(2)}, u32[]{:S(2)}) collective-permute-start(bf16[48,2176]{1,0:T(8,128)(2,1)S(1)} %collective-permute-done.1.refs_2_), channel_id=1, source_target_pairs={{0,224},{32,0},{64,32},{96,64},{128,96},{160,128},{192,160},{224,1... | collective-permute-start | bytes 626696 | tf_op jit(solution)/shard_map/ppermute | solution.py:45
  25.2 7.9 %collective-permute-start.6 = (bf16[48,2176]{1,0:T(8,128)(2,1)S(1)}, bf16[48,2176]{1,0:T(8,128)(2,1)S(1)}, u32[]{:S(2)}, u32[]{:S(2)}) collective-permute-start(bf16[48,2176]{1,0:T(8,128)(2,1)S(1)} %collective-permute-done.5.refs_0_.refs_5_), channel_id=1, source_target_pairs={{0,32},{32,64},{64,96},{96,128},{128,160},{160,192},{192,224},{224... | collective-permute-start | bytes 626696 | tf_op jit(solution)/shard_map/ppermute | solution.py:42
  25.2 1.0 copy-start.6
  26.2 6.9 %collective-permute-start.7 = (bf16[48,2048]{1,0:T(8,128)(2,1)S(1)}, bf16[48,2048]{1,0:T(8,128)(2,1)S(1)}, u32[]{:S(2)}, u32[]{:S(2)}) collective-permute-start(bf16[48,2048]{1,0:T(8,128)(2,1)S(1)} %narrow.1.refs_0_), channel_id=1, source_target_pairs={{0,224},{32,0},{64,32},{96,64},{128,96},{160,128},{192,160},{224,1... | collective-permute-start | bytes 589832 | tf_op jit(solution)/shard_map/ppermute | solution.py:42
  33.1 0.9 copy-start.5
  36.5 34.0 %all-to-all-start = ((bf16[16,32,2048]{2,1,0:T(8,128)(2,1)}), bf16[16,32,2048]{2,1,0:T(8,128)(2,1)S(1)}, u32[]{:S(2)}, u32[]{:S(2)}) async-start(bf16[16,32,2048]{2,1,0:T(8,128)(2,1)} %bitcast.44), calls=%async_computation | async-start | bytes 4194304 | tf_op jit(solution)/shard_map/all_to_all | solution.py:350
  43.6 7.0 %collective-permute-start.11 = (bf16[48,2048]{1,0:T(8,128)(2,1)S(1)}, bf16[48,2048]{1,0:T(8,128)(2,1)S(1)}, u32[]{:S(2)}, u32[]{:S(2)}) collective-permute-start(bf16[48,2048]{1,0:T(8,128)(2,1)S(1)} %narrow.1.refs_0_), channel_id=1, source_target_pairs={{0,32},{32,64},{64,96},{96,128},{128,160},{160,192},{192,224},{224... | collective-permute-start | bytes 589832 | tf_op jit(solution)/shard_map/ppermute | solution.py:45
  47.4 7.3 %collective-permute-start.8 = (bf16[48,2048]{1,0:T(8,128)(2,1)S(1)}, bf16[48,2048]{1,0:T(8,128)(2,1)S(1)}, u32[]{:S(2)}, u32[]{:S(2)}) collective-permute-start(bf16[48,2048]{1,0:T(8,128)(2,1)S(1)} %collective-permute-done.7.refs_8_.refs_1_), channel_id=1, source_target_pairs={{0,224},{32,0},{64,32},{96,64},{128,96},{160,128},{192,160},{224,1... | collective-permute-start | bytes 589832 | tf_op jit(solution)/shard_map/ppermute | solution.py:42
  47.4 30.6 %collective-permute-start.15 = (bf16[2048,384]{1,0:T(8,128)(2,1)}, bf16[2048,384]{1,0:T(8,128)(2,1)}, u32[]{:S(2)}, u32[]{:S(2)}) collective-permute-start(bf16[2048,384]{1,0:T(8,128)(2,1)} %bitcast.45), channel_id=1, source_target_pairs={{0,1},{1,0},{2,3},{3,2},{4,5},{5,4},{6,7},{7,6},{8,9},{9,8},{10,11... | collective-permute-start | bytes 4718600 | tf_op jit(solution)/shard_map/ppermute | solution.py:367
  50.6 6.9 %collective-permute-start.12 = (bf16[48,2048]{1,0:T(8,128)(2,1)S(1)}, bf16[48,2048]{1,0:T(8,128)(2,1)S(1)}, u32[]{:S(2)}, u32[]{:S(2)}) collective-permute-start(bf16[48,2048]{1,0:T(8,128)(2,1)S(1)} %collective-permute-done.11.refs_7_), channel_id=1, source_target_pairs={{0,32},{32,64},{64,96},{96,128},{128,160},{160,192},{192,224},{224... | collective-permute-start | bytes 589832 | tf_op jit(solution)/shard_map/ppermute | solution.py:45
  54.7 6.4 %collective-permute-start.9 = (bf16[48,2048]{1,0:T(8,128)(2,1)S(1)}, bf16[48,2048]{1,0:T(8,128)(2,1)S(1)}, u32[]{:S(2)}, u32[]{:S(2)}) collective-permute-start(bf16[48,2048]{1,0:T(8,128)(2,1)S(1)} %collective-permute-done.8.refs_2_), channel_id=1, source_target_pairs={{0,224},{32,0},{64,32},{96,64},{128,96},{160,128},{192,160},{224,1... | collective-permute-start | bytes 589832 | tf_op jit(solution)/shard_map/ppermute | solution.py:42
  54.7 25.5 %collective-permute-start.16 = (bf16[2048,384]{1,0:T(8,128)(2,1)}, bf16[2048,384]{1,0:T(8,128)(2,1)}, u32[]{:S(2)}, u32[]{:S(2)}) collective-permute-start(bf16[2048,384]{1,0:T(8,128)(2,1)} %bitcast.47), channel_id=1, source_target_pairs={{0,1},{1,0},{2,3},{3,2},{4,5},{5,4},{6,7},{7,6},{8,9},{9,8},{10,11... | collective-permute-start | bytes 4718600 | tf_op jit(solution)/shard_map/ppermute | solution.py:367
  57.5 6.9 %collective-permute-start.13 = (bf16[48,2048]{1,0:T(8,128)(2,1)S(1)}, bf16[48,2048]{1,0:T(8,128)(2,1)S(1)}, u32[]{:S(2)}, u32[]{:S(2)}) collective-permute-start(bf16[48,2048]{1,0:T(8,128)(2,1)S(1)} %collective-permute-done.12.refs_6_), channel_id=1, source_target_pairs={{0,32},{32,64},{64,96},{96,128},{128,160},{160,192},{192,224},{224... | collective-permute-start | bytes 589832 | tf_op jit(solution)/shard_map/ppermute | solution.py:45
  61.1 6.0 %collective-permute-start.10 = (bf16[48,2048]{1,0:T(8,128)(2,1)S(1)}, bf16[48,2048]{1,0:T(8,128)(2,1)S(1)}, u32[]{:S(2)}, u32[]{:S(2)}) collective-permute-start(bf16[48,2048]{1,0:T(8,128)(2,1)S(1)} %collective-permute-done.9.refs_3_), channel_id=1, source_target_pairs={{0,224},{32,0},{64,32},{96,64},{128,96},{160,128},{192,160},{224,1... | collective-permute-start | bytes 589832 | tf_op jit(solution)/shard_map/ppermute | solution.py:42
  70.6 1.4 copy-start.2
  72.0 32.7 %all-to-all-start.1 = ((bf16[16,32,2048]{2,1,0:T(8,128)(2,1)}), bf16[16,32,2048]{2,1,0:T(8,128)(2,1)}, u32[]{:S(2)}, u32[]{:S(2)}) async-start(bf16[16,32,2048]{2,1,0:T(8,128)(2,1)} %bitcast.43), calls=%async_computation.1 | async-start | bytes 4194304 | tf_op jit(solution)/shard_map/all_to_all | solution.py:350
  77.9 2.4 %copy-start.7 = (bf16[1,2048,384]{2,1,0:T(8,128)(2,1)S(1)}, bf16[1,2048,384]{2,1,0:T(8,128)(2,1)}, u32[]{:S(2)}) copy-start(bf16[1,2048,384]{2,1,0:T(8,128)(2,1)} %param.12) | copy-start | bytes 4718596
  77.9 5.2 %collective-permute-start.14 = (bf16[2048,384]{1,0:T(8,128)(2,1)}, bf16[2048,384]{1,0:T(8,128)(2,1)S(1)}, u32[]{:S(2)}, u32[]{:S(2)}) collective-permute-start(bf16[2048,384]{1,0:T(8,128)(2,1)} %bitcast.49), channel_id=1, source_target_pairs={{0,1},{1,0},{2,3},{3,2},{4,5},{5,4},{6,7},{7,6},{8,9},{9,8},{10,11... | collective-permute-start | bytes 4718600 | tf_op jit(solution)/shard_map/ppermute | solution.py:367
  80.2 5.0 %copy-start = (bf16[2048,768]{1,0:T(8,128)(2,1)}, bf16[2048,768]{1,0:T(8,128)(2,1)S(1)}, u32[]{:S(2)}) copy-start(bf16[2048,768]{1,0:T(8,128)(2,1)S(1)} %pad_maximum_fusion.1.wg_ref.wg_h) | copy-start | bytes 9437188
  80.2 3.0 %copy-start.8 = (bf16[1,2048,384]{2,1,0:T(8,128)(2,1)S(1)}, bf16[1,2048,384]{2,1,0:T(8,128)(2,1)}, u32[]{:S(2)}) copy-start(bf16[1,2048,384]{2,1,0:T(8,128)(2,1)} %param.13) | copy-start | bytes 4718596
  83.1 2.9 %copy-start.1 = (bf16[2048,768]{1,0:T(8,128)(2,1)}, bf16[2048,768]{1,0:T(8,128)(2,1)S(1)}, u32[]{:S(2)}) copy-start(bf16[2048,768]{1,0:T(8,128)(2,1)S(1)} %pad_maximum_fusion.2.wu_ref.wu_h) | copy-start | bytes 9437188
  83.1 3.2 %copy-start.3 = (bf16[16,32,2048]{2,1,0:T(8,128)(2,1)S(1)}, bf16[16,32,2048]{2,1,0:T(8,128)(2,1)}, u32[]{:S(2)}) copy-start(bf16[16,32,2048]{2,1,0:T(8,128)(2,1)} %copy-done.2) | copy-start | bytes 6291460
  115.5 8.5 %copy-start.11 = (bf16[512,768]{1,0:T(8,128)(2,1)S(1)}, bf16[512,768]{1,0:T(8,128)(2,1)}, u32[]{:S(2)}) copy-start(bf16[512,768]{1,0:T(8,128)(2,1)} %get-tuple-element.23) | copy-start | bytes 2359300
  115.5 58.5 %all-to-all-start.2 = ((bf16[128,4,2048]{2,1,0:T(4,128)(2,1)}), bf16[128,4,2048]{2,1,0:T(4,128)(2,1)S(1)}, u32[]{:S(2)}, u32[]{:S(2)}) async-start(bf16[128,4,2048]{2,1,0:T(4,128)(2,1)} %get-tuple-element.20), calls=%async_computation.2 | async-start | bytes 4194304 | tf_op jit(solution)/shard_map/all_to_all | solution.py:373
  124.0 3.2 %copy-start.4 = (bf16[16,32,2048]{2,1,0:T(8,128)(2,1)S(1)}, bf16[16,32,2048]{2,1,0:T(8,128)(2,1)}, u32[]{:S(2)}) copy-start(bf16[16,32,2048]{2,1,0:T(8,128)(2,1)} %copy-done.2) | copy-start | bytes 6291460
  124.0 3.2 %copy-start.12 = (bf16[512,768]{1,0:T(8,128)(2,1)S(1)}, bf16[512,768]{1,0:T(8,128)(2,1)}, u32[]{:S(2)}) copy-start(bf16[512,768]{1,0:T(8,128)(2,1)} %get-tuple-element.22) | copy-start | bytes 2359300
  127.1 3.9 %collective-permute-start.19 = (bf16[2048,384]{1,0:T(8,128)(2,1)S(1)}, bf16[2048,384]{1,0:T(8,128)(2,1)S(1)}, u32[]{:S(2)}, u32[]{:S(2)}) collective-permute-start(bf16[2048,384]{1,0:T(8,128)(2,1)S(1)} %convolution_convert_fusion), channel_id=1, source_target_pairs={{0,1},{1,0},{2,3},{3,2},{4,5},{5,4},{6,7},{7,6},{8,9},{9,8},{10,11... | collective-permute-start | bytes 4718600 | tf_op jit(solution)/shard_map/ppermute | solution.py:378
  127.2 1.9 %copy-start.10 = (bf16[512,768]{1,0:T(8,128)(2,1)S(1)}, bf16[512,768]{1,0:T(8,128)(2,1)}, u32[]{:S(2)}) copy-start(bf16[512,768]{1,0:T(8,128)(2,1)} %get-tuple-element.21) | copy-start | bytes 2359300
  128.5 6.5 %collective-permute-start.18 = (bf16[2048,384]{1,0:T(8,128)(2,1)S(1)}, bf16[2048,384]{1,0:T(8,128)(2,1)S(1)}, u32[]{:S(2)}, u32[]{:S(2)}) collective-permute-start(bf16[2048,384]{1,0:T(8,128)(2,1)S(1)} %convolution_convert_fusion.2), channel_id=1, source_target_pairs={{0,1},{1,0},{2,3},{3,2},{4,5},{5,4},{6,7},{7,6},{8,9},{9,8},{10,11... | collective-permute-start | bytes 4718600 | tf_op jit(solution)/shard_map/ppermute | solution.py:378
  129.1 1.5 copy-start.9
  130.4 7.2 %collective-permute-start.17 = (bf16[2048,384]{1,0:T(8,128)(2,1)S(1)}, bf16[2048,384]{1,0:T(8,128)(2,1)S(1)}, u32[]{:S(2)}, u32[]{:S(2)}) collective-permute-start(bf16[2048,384]{1,0:T(8,128)(2,1)S(1)} %convolution_convert_fusion.4), channel_id=1, source_target_pairs={{0,1},{1,0},{2,3},{3,2},{4,5},{5,4},{6,7},{7,6},{8,9},{9,8},{10,11... | collective-permute-start | bytes 4718600 | tf_op jit(solution)/shard_map/ppermute | solution.py:378

commit v2 on v1

--- a/solution.py
+++ b/solution.py
@@ -270,18 +270,17 @@
 
         go_in.start()
         wd_in[0].start()
-        slope_in.start()
-        act_in.start()
         go_in.wait()
         wd_in[0].wait()
-        for copy in wd_in[1:] + later:
+        for copy in [slope_in, act_in] + wd_in[1:] + later:
             copy.start()
-        slope_in.wait()
-        act_in.wait()
         for i in range(0, hidden, part):
             if i > 0:
                 wd_in[i // part].wait()
             dh = mm(go_ref[...], wd_ref[:, i : i + part], ((1,), (0,)))
+            if i == 0:
+                slope_in.wait()
+                act_in.wait()
             da_ref[:, i : i + part] = (dh * slope_ref[:, i : i + part]).astype(BF16)
             db_ref[:, i : i + part] = (dh * act_ref[:, i : i + part]).astype(BF16)
         for copy in keep:

time: 176 us -> 176 us (level)
  no operation moved by 1% of the time
where the time goes in v2:
time: 176 us
  waiting for transfers between devices  79 us (45%)
  starting transfers between devices  44.4 us (25%)
  Pallas kernels  24.8 us (14%)
  matrix products  15.1 us (9%)
  other arithmetic  7.01 us (4%)
  local copies, waits for them, and re-layouts  4.57 us (3%)
    all_to_all x1, waiting for transfers between devices, per_device(): lax.all_to_all(dxs, ('y', 'x', 'z'), split_axis=0, concat_axis=0, tiled=T...  34 us
    ppermute x8, waiting for transfers between devices, along_z(): lax.ppermute(ahead, 'z', [(i, (i + first) % depth) for i in range(depth)])  21.3 us
    dot_general x7, matrix products, mm(): lax.dot_general(a, b, ((dims[0], dims[1]), ((), ())), preferred_element_t...  15.1 us
    ppermute x6, starting transfers between devices, along_z(): lax.ppermute(behind, 'z', [(i, (i - first) % depth) for i in range(depth)])  15 us
    all_to_all x2, waiting for transfers between devices, in_plane(): lax.all_to_all(rows.reshape(PLANE, block, width), ('y', 'x'), split_axis=...  14.1 us
    all_to_all x2, starting transfers between devices, in_plane(): lax.all_to_all(rows.reshape(PLANE, block, width), ('y', 'x'), split_axis=...  12.9 us
    pallas_call x1, Pallas kernels, backward(): pl.pallas_call(body, in_specs=[IN_HBM] * 6, out_specs=[IN_HBM] * 3, out_s...  11.3 us
    ppermute x6, waiting for transfers between devices, along_z(): lax.ppermute(behind, 'z', [(i, (i - first) % depth) for i in range(depth)])  9.63 us
  transfers between devices with their start and end apart: 23, of which 14 were waited for; matrix products, arithmetic and copies ran while one was open for 13% of the time, Pallas kernels for 4%

profile of v2, /device:TPU:32, one launch (start us, length us, event | category | flops | bytes accessed | tf_op | source)
XLA Modules:
  0.0 175.8 jit_solution(4361543374871352134)
XLA Ops:
  0.6 1.9 %prepare.1.refs_0_ = bf16[48,2176]{1,0:T(8,128)(2,1)} custom-call(f32[48,2048]{1,0:T(8,128)} %x_ref.2, s32[8,48]{1,0:T(8,128)} %bitcast.51, f32[8,48]{1,0:T(8,128)} %bitcast.53), custom_call_target="tpu_custom_call" | custom-call | tf_op jit(solution)/shard_map/prepare/pallas_call | solution.py:64
  2.5 1.9 %collective-permute-start.3 = (bf16[48,2176]{1,0:T(8,128)(2,1)}, bf16[48,2176]{1,0:T(8,128)(2,1)S(1)}, u32[]{:S(2)}, u32[]{:S(2)}) collective-permute-start(bf16[48,2176]{1,0:T(8,128)(2,1)} %prepare.1.refs_0_), channel_id=1, source_target_pairs={{0,32},{32,64},{64,96},{96,128},{128,160},{160,192},{192,224},{224... | collective-permute-start | bytes 626696 | tf_op jit(solution)/shard_map/ppermute | solution.py:42
  4.5 5.1 %collective-permute-done.3.refs_7_ = bf16[48,2176]{1,0:T(8,128)(2,1)S(1)} collective-permute-done((bf16[48,2176]{1,0:T(8,128)(2,1)}, bf16[48,2176]{1,0:T(8,128)(2,1)S(1)}, u32[]{:S(2)}, u32[]{:S(2)}) %collective-permute-start.3) | collective-permute-done | bytes 208928 | tf_op jit(solution)/shard_map/ppermute | solution.py:42
  9.6 1.9 %collective-permute-start.4 = (bf16[48,2176]{1,0:T(8,128)(2,1)S(1)}, bf16[48,2176]{1,0:T(8,128)(2,1)S(1)}, u32[]{:S(2)}, u32[]{:S(2)}) collective-permute-start(bf16[48,2176]{1,0:T(8,128)(2,1)S(1)} %collective-permute-done.3.refs_7_), channel_id=1, source_target_pairs={{0,32},{32,64},{64,96},{96,128},{128,160},{160,192},{192,224},{224... | collective-permute-start | bytes 626696 | tf_op jit(solution)/shard_map/ppermute | solution.py:42
  11.5 2.3 %collective-permute-start.1 = (bf16[48,2176]{1,0:T(8,128)(2,1)S(1)}, bf16[48,2176]{1,0:T(8,128)(2,1)S(1)}, u32[]{:S(2)}, u32[]{:S(2)}) collective-permute-start(bf16[48,2176]{1,0:T(8,128)(2,1)S(1)} %collective-permute-done.refs_1_), channel_id=1, source_target_pairs={{0,224},{32,0},{64,32},{96,64},{128,96},{160,128},{192,160},{224,1... | collective-permute-start | bytes 626696 | tf_op jit(solution)/shard_map/ppermute | solution.py:45
  13.9 4.6 %collective-permute-done.4.refs_6_ = bf16[48,2176]{1,0:T(8,128)(2,1)S(1)} collective-permute-done((bf16[48,2176]{1,0:T(8,128)(2,1)S(1)}, bf16[48,2176]{1,0:T(8,128)(2,1)S(1)}, u32[]{:S(2)}, u32[]{:S(2)}) %collective-permute-start.4) | collective-permute-done | bytes 208928 | tf_op jit(solution)/shard_map/ppermute | solution.py:42
  18.5 0.4 collective-permute-done.1.refs_2_
  18.9 2.5 %collective-permute-start.2 = (bf16[48,2176]{1,0:T(8,128)(2,1)S(1)}, bf16[48,2176]{1,0:T(8,128)(2,1)S(1)}, u32[]{:S(2)}, u32[]{:S(2)}) collective-permute-start(bf16[48,2176]{1,0:T(8,128)(2,1)S(1)} %collective-permute-done.1.refs_2_), channel_id=1, source_target_pairs={{0,224},{32,0},{64,32},{96,64},{128,96},{160,128},{192,160},{224,1... | collective-permute-start | bytes 626696 | tf_op jit(solution)/shard_map/ppermute | solution.py:45
  21.4 3.8 %collective-permute-done.5.refs_0_.refs_5_ = bf16[48,2176]{1,0:T(8,128)(2,1)S(1)} collective-permute-done((bf16[48,2176]{1,0:T(8,128)(2,1)S(1)}, bf16[48,2176]{1,0:T(8,128)(2,1)S(1)}, u32[]{:S(2)}, u32[]{:S(2)}) %collective-permute-start.5) | collective-permute-done | bytes 208928 | tf_op jit(solution)/shard_map/ppermute | solution.py:42
  25.2 1.0 copy-done.6
  26.2 3.3 %collective-permute-start.7 = (bf16[48,2048]{1,0:T(8,128)(2,1)S(1)}, bf16[48,2048]{1,0:T(8,128)(2,1)S(1)}, u32[]{:S(2)}, u32[]{:S(2)}) collective-permute-start(bf16[48,2048]{1,0:T(8,128)(2,1)S(1)} %narrow.1.refs_0_), channel_id=1, source_target_pairs={{0,224},{32,0},{64,32},{96,64},{128,96},{160,128},{192,160},{224,1... | collective-permute-start | bytes 589832 | tf_op jit(solution)/shard_map/ppermute | solution.py:42
  29.5 3.6 %collective-permute-done.7.refs_8_.refs_1_ = bf16[48,2048]{1,0:T(8,128)(2,1)S(1)} collective-permute-done((bf16[48,2048]{1,0:T(8,128)(2,1)S(1)}, bf16[48,2048]{1,0:T(8,128)(2,1)S(1)}, u32[]{:S(2)}, u32[]{:S(2)}) %collective-permute-start.7) | collective-permute-done | bytes 196640 | tf_op jit(solution)/shard_map/ppermute | solution.py:42
  33.1 0.9 copy-done.5
  34.0 2.5 %fill_x.1 = (bf16[512,2048]{1,0:T(8,128)(2,1)}, bf16[512,384]{1,0:T(8,128)(2,1)S(1)}) custom-call(s32[1]{0:T(128)} %bitcast.9.z_ref, bf16[48,2176]{1,0:T(8,128)(2,1)S(1)} %copy-done.5, bf16[48,2176]{1,0:T(8,128)(2,1)S(1)} %collective-permute-done.refs_1_, bf16[48,2176]{1,0:T(8,128)(2,1)S(1)} %collective-permute-done.1.refs_2_, ...), custom_call_target="tpu_custom_call" | custom-call | tf_op jit(solution)/shard_map/fill_x/pallas_call | solution.py:137
  36.5 7.0 %all-to-all-start = ((bf16[16,32,2048]{2,1,0:T(8,128)(2,1)}), bf16[16,32,2048]{2,1,0:T(8,128)(2,1)S(1)}, u32[]{:S(2)}, u32[]{:S(2)}) async-start(bf16[16,32,2048]{2,1,0:T(8,128)(2,1)} %bitcast.44), calls=%async_computation | async-start | bytes 4194304 | tf_op jit(solution)/shard_map/all_to_all | solution.py:349
  43.6 3.8 %collective-permute-start.11 = (bf16[48,2048]{1,0:T(8,128)(2,1)S(1)}, bf16[48,2048]{1,0:T(8,128)(2,1)S(1)}, u32[]{:S(2)}, u32[]{:S(2)}) collective-permute-start(bf16[48,2048]{1,0:T(8,128)(2,1)S(1)} %narrow.1.refs_0_), channel_id=1, source_target_pairs={{0,32},{32,64},{64,96},{96,128},{128,160},{160,192},{192,224},{224... | collective-permute-start | bytes 589832 | tf_op jit(solution)/shard_map/ppermute | solution.py:45
  47.4 3.2 %collective-permute-done.11.refs_7_ = bf16[48,2048]{1,0:T(8,128)(2,1)S(1)} collective-permute-done((bf16[48,2048]{1,0:T(8,128)(2,1)S(1)}, bf16[48,2048]{1,0:T(8,128)(2,1)S(1)}, u32[]{:S(2)}, u32[]{:S(2)}) %collective-permute-start.11) | collective-permute-done | bytes 196640 | tf_op jit(solution)/shard_map/ppermute | solution.py:45
  50.6 3.7 %collective-permute-start.12 = (bf16[48,2048]{1,0:T(8,128)(2,1)S(1)}, bf16[48,2048]{1,0:T(8,128)(2,1)S(1)}, u32[]{:S(2)}, u32[]{:S(2)}) collective-permute-start(bf16[48,2048]{1,0:T(8,128)(2,1)S(1)} %collective-permute-done.11.refs_7_), channel_id=1, source_target_pairs={{0,32},{32,64},{64,96},{96,128},{128,160},{160,192},{192,224},{224... | collective-permute-start | bytes 589832 | tf_op jit(solution)/shard_map/ppermute | solution.py:45
  54.3 0.5 collective-permute-done.8.refs_2_
  54.7 2.8 %collective-permute-done.12.refs_6_ = bf16[48,2048]{1,0:T(8,128)(2,1)S(1)} collective-permute-done((bf16[48,2048]{1,0:T(8,128)(2,1)S(1)}, bf16[48,2048]{1,0:T(8,128)(2,1)S(1)}, u32[]{:S(2)}, u32[]{:S(2)}) %collective-permute-start.12) | collective-permute-done | bytes 196640 | tf_op jit(solution)/shard_map/ppermute | solution.py:45
  57.5 2.6 %collective-permute-start.13 = (bf16[48,2048]{1,0:T(8,128)(2,1)S(1)}, bf16[48,2048]{1,0:T(8,128)(2,1)S(1)}, u32[]{:S(2)}, u32[]{:S(2)}) collective-permute-start(bf16[48,2048]{1,0:T(8,128)(2,1)S(1)} %collective-permute-done.12.refs_6_), channel_id=1, source_target_pairs={{0,32},{32,64},{64,96},{96,128},{128,160},{160,192},{192,224},{224... | collective-permute-start | bytes 589832 | tf_op jit(solution)/shard_map/ppermute | solution.py:45
  60.1 1.1 collective-permute-done.9.refs_3_
  61.1 3.2 %collective-permute-done.13.refs_5_ = bf16[48,2048]{1,0:T(8,128)(2,1)S(1)} collective-permute-done((bf16[48,2048]{1,0:T(8,128)(2,1)S(1)}, bf16[48,2048]{1,0:T(8,128)(2,1)S(1)}, u32[]{:S(2)}, u32[]{:S(2)}) %collective-permute-start.13) | collective-permute-done | bytes 196640 | tf_op jit(solution)/shard_map/ppermute | solution.py:45
  64.4 2.7 %collective-permute-done.10.refs_4_ = bf16[48,2048]{1,0:T(8,128)(2,1)S(1)} collective-permute-done((bf16[48,2048]{1,0:T(8,128)(2,1)S(1)}, bf16[48,2048]{1,0:T(8,128)(2,1)S(1)}, u32[]{:S(2)}, u32[]{:S(2)}) %collective-permute-start.10) | collective-permute-done | bytes 196640 | tf_op jit(solution)/shard_map/ppermute | solution.py:42
  67.1 2.2 %fill_g.1 = bf16[512,2048]{1,0:T(8,128)(2,1)} custom-call(bf16[512,384]{1,0:T(8,128)(2,1)S(1)} %get-tuple-element.14.weigh_ref, bf16[48,2048]{1,0:T(8,128)(2,1)S(1)} %narrow.1.refs_0_, bf16[48,2048]{1,0:T(8,128)(2,1)S(1)} %collective-permute-done.7.refs_8_.refs_1_, bf16[48,2048]{1,0:T(8,128)(2,1)S(1)} %collective-permute-done.8.refs_2_, ...), custom_call_target="tpu_custom_call" | custom-call | tf_op jit(solution)/shard_map/fill_g/pallas_call | solution.py:171
  69.3 1.3 all-to-all-done
  70.6 1.4 copy-done.2
  72.0 5.9 %all-to-all-start.1 = ((bf16[16,32,2048]{2,1,0:T(8,128)(2,1)}), bf16[16,32,2048]{2,1,0:T(8,128)(2,1)}, u32[]{:S(2)}, u32[]{:S(2)}) async-start(bf16[16,32,2048]{2,1,0:T(8,128)(2,1)} %bitcast.43), calls=%async_computation.1 | async-start | bytes 4194304 | tf_op jit(solution)/shard_map/all_to_all | solution.py:349
  78.0 2.2 %pad_maximum_fusion.1.wg_ref.wg_h = bf16[2048,768]{1,0:T(8,128)(2,1)S(1)} fusion(bf16[2048,384]{1,0:T(8,128)(2,1)} %collective-permute-done.15, bf16[2048,384]{1,0:T(8,128)(2,1)} %bitcast.46), kind=kLoop, calls=%fused_computation.1 | loop fusion | flops 6291456 | bytes 6291456 | tf_op jit(solution)/shard_map/concatenate | solution.py:366
  80.3 2.8 %pad_maximum_fusion.2.wu_ref.wu_h = bf16[2048,768]{1,0:T(8,128)(2,1)S(1)} fusion(bf16[2048,384]{1,0:T(8,128)(2,1)} %collective-permute-done.16, bf16[2048,384]{1,0:T(8,128)(2,1)S(1)} %bitcast.48), kind=kLoop, calls=%fused_computation.2 | loop fusion | flops 6291456 | bytes 6291456 | tf_op jit(solution)/shard_map/concatenate | solution.py:366
  83.1 0.1 copy-done.8
  83.2 1.9 %pad_maximum_fusion.wd_h = bf16[2048,768]{1,0:T(8,128)(2,1)} fusion(bf16[2048,384]{1,0:T(8,128)(2,1)S(1)} %collective-permute-done.14, bf16[2048,384]{1,0:T(8,128)(2,1)S(1)} %bitcast.50), kind=kLoop, calls=%fused_computation | loop fusion | flops 6291456 | bytes 6291456 | tf_op jit(solution)/shard_map/concatenate | solution.py:366
  85.2 0.7 copy-done.1
  85.9 0.3 copy-done.3
  86.3 5.6 %activations.1 = (f32[512,768]{1,0:T(8,128)}, f32[512,768]{1,0:T(8,128)}, bf16[512,768]{1,0:T(8,128)(2,1)}) custom-call(bf16[512,2048]{1,0:T(8,128)(2,1)S(1)} %bitcast.38, bf16[2048,768]{1,0:T(8,128)(2,1)S(1)} %pad_maximum_fusion.1.wg_ref.wg_h, bf16[2048,768]{1,0:T(8,128)(2,1)S(1)} %pad_maximum_fusion.2.wu_ref.wu_h), custom_call_target="tpu_custom_call" | custom-call | tf_op jit(solution)/shard_map/activations/pallas_call | solution.py:204
  91.9 12.8 %all-to-all-done.1 = bf16[16,32,2048]{2,1,0:T(8,128)(2,1)} async-done(((bf16[16,32,2048]{2,1,0:T(8,128)(2,1)}), bf16[16,32,2048]{2,1,0:T(8,128)(2,1)}, u32[]{:S(2)}, u32[]{:S(2)}) %all-to-all-start.1) | async-done | bytes 2097184 | tf_op jit(solution)/shard_map/all_to_all | solution.py:349
  104.7 11.3 %backward.1 = (bf16[128,4,2048]{2,1,0:T(4,128)(2,1)}, bf16[512,768]{1,0:T(8,128)(2,1)}, bf16[512,768]{1,0:T(8,128)(2,1)}) custom-call(bf16[512,2048]{1,0:T(8,128)(2,1)} %bitcast.14.go_h, bf16[2048,768]{1,0:T(8,128)(2,1)} %pad_maximum_fusion.wd_h, f32[512,768]{1,0:T(8,128)} %get-tuple-element.18.act_h, f32[512,768]{1,0:T(8,128)} %get-tuple-element.19.slope_h, ...), custom_call_target="tpu_custom_call" | custom-call | tf_op jit(solution)/shard_map/backward/pallas_call | solution.py:301
  116.0 8.5 %all-to-all-start.2 = ((bf16[128,4,2048]{2,1,0:T(4,128)(2,1)}), bf16[128,4,2048]{2,1,0:T(4,128)(2,1)S(1)}, u32[]{:S(2)}, u32[]{:S(2)}) async-start(bf16[128,4,2048]{2,1,0:T(4,128)(2,1)} %get-tuple-element.20), calls=%async_computation.2 | async-start | bytes 4194304 | tf_op jit(solution)/shard_map/all_to_all | solution.py:372
  124.5 3.0 %convolution_convert_fusion = bf16[2048,384]{1,0:T(8,128)(2,1)S(1)} fusion(bf16[512,2048]{1,0:T(8,128)(2,1)} %bitcast.14.go_h, bf16[512,768]{1,0:T(8,128)(2,1)S(1)} %copy-done.11), kind=kOutput, calls=%fused_computation.6 | convolution fusion | flops 806092800 | bytes 4063232 | tf_op jit(solution)/shard_map/dot_general | solution.py:18
  127.7 1.3 convolution_convert_fusion.2
  129.0 0.6 collective-permute-start.18
  129.5 1.3 convolution_convert_fusion.4
  131.0 0.4 fusion.4.pick_ref
  131.4 4.1 %fusion.2 = bf16[1,2048,384]{2,1,0:T(8,128)(2,1)} fusion(bf16[2048,384]{1,0:T(8,128)(2,1)S(1)} %collective-permute-done.19, bf16[512,2048]{1,0:T(8,128)(2,1)} %bitcast.14.go_h, bf16[512,768]{1,0:T(8,128)(2,1)S(1)} %copy-done.11), kind=kOutput, calls=%fused_computation.14 | convolution fusion | flops 809238528 | bytes 5636096 | tf_op jit(solution)/shard_map/dot_general | solution.py:18
  135.5 2.5 %fusion.1 = bf16[1,2048,384]{2,1,0:T(8,128)(2,1)} fusion(bf16[2048,384]{1,0:T(8,128)(2,1)S(1)} %collective-permute-done.18, bf16[512,2048]{1,0:T(8,128)(2,1)S(1)} %bitcast.41, bf16[512,768]{1,0:T(8,128)(2,1)S(1)} %copy-done.12), kind=kOutput, calls=%fused_computation.13 | convolution fusion | flops 809238528 | bytes 5636096 | tf_op jit(solution)/shard_map/dot_general | solution.py:18
  138.0 2.5 %fusion = bf16[1,2048,384]{2,1,0:T(8,128)(2,1)} fusion(bf16[2048,384]{1,0:T(8,128)(2,1)S(1)} %collective-permute-done.17, bf16[512,2048]{1,0:T(8,128)(2,1)S(1)} %bitcast.42, bf16[512,768]{1,0:T(8,128)(2,1)S(1)} %copy-done.10), kind=kOutput, calls=%fused_computation.12 | convolution fusion | flops 809238528 | bytes 5636096 | tf_op jit(solution)/shard_map/dot_general | solution.py:18
  140.5 34.0 %all-to-all-done.2.rows_ref = bf16[128,4,2048]{2,1,0:T(4,128)(2,1)S(1)} async-done(((bf16[128,4,2048]{2,1,0:T(4,128)(2,1)}), bf16[128,4,2048]{2,1,0:T(4,128)(2,1)S(1)}, u32[]{:S(2)}, u32[]{:S(2)}) %all-to-all-start.2) | async-done | bytes 2097184 | tf_op jit(solution)/shard_map/all_to_all | solution.py:372
  174.5 1.3 combine.1
  (45 shorter events, 0.6 us)
Async XLA Ops:
  2.5 7.1 %collective-permute-start.3 = (bf16[48,2176]{1,0:T(8,128)(2,1)}, bf16[48,2176]{1,0:T(8,128)(2,1)S(1)}, u32[]{:S(2)}, u32[]{:S(2)}) collective-permute-start(bf16[48,2176]{1,0:T(8,128)(2,1)} %prepare.1.refs_0_), channel_id=1, source_target_pairs={{0,32},{32,64},{64,96},{96,128},{128,160},{160,192},{192,224},{224... | collective-permute-start | bytes 626696 | tf_op jit(solution)/shard_map/ppermute | solution.py:42
  4.4 7.1 %collective-permute-start = (bf16[48,2176]{1,0:T(8,128)(2,1)}, bf16[48,2176]{1,0:T(8,128)(2,1)S(1)}, u32[]{:S(2)}, u32[]{:S(2)}) collective-permute-start(bf16[48,2176]{1,0:T(8,128)(2,1)} %prepare.1.refs_0_), channel_id=1, source_target_pairs={{0,224},{32,0},{64,32},{96,64},{128,96},{160,128},{192,160},{224,1... | collective-permute-start | bytes 626696 | tf_op jit(solution)/shard_map/ppermute | solution.py:45
  9.6 8.8 %collective-permute-start.4 = (bf16[48,2176]{1,0:T(8,128)(2,1)S(1)}, bf16[48,2176]{1,0:T(8,128)(2,1)S(1)}, u32[]{:S(2)}, u32[]{:S(2)}) collective-permute-start(bf16[48,2176]{1,0:T(8,128)(2,1)S(1)} %collective-permute-done.3.refs_7_), channel_id=1, source_target_pairs={{0,32},{32,64},{64,96},{96,128},{128,160},{160,192},{192,224},{224... | collective-permute-start | bytes 626696 | tf_op jit(solution)/shard_map/ppermute | solution.py:42
  11.5 7.3 %collective-permute-start.1 = (bf16[48,2176]{1,0:T(8,128)(2,1)S(1)}, bf16[48,2176]{1,0:T(8,128)(2,1)S(1)}, u32[]{:S(2)}, u32[]{:S(2)}) collective-permute-start(bf16[48,2176]{1,0:T(8,128)(2,1)S(1)} %collective-permute-done.refs_1_), channel_id=1, source_target_pairs={{0,224},{32,0},{64,32},{96,64},{128,96},{160,128},{192,160},{224,1... | collective-permute-start | bytes 626696 | tf_op jit(solution)/shard_map/ppermute | solution.py:45
  18.5 6.7 %collective-permute-start.5 = (bf16[48,2176]{1,0:T(8,128)(2,1)S(1)}, bf16[48,2176]{1,0:T(8,128)(2,1)S(1)}, u32[]{:S(2)}, u32[]{:S(2)}) collective-permute-start(bf16[48,2176]{1,0:T(8,128)(2,1)S(1)} %collective-permute-done.4.refs_6_), channel_id=1, source_target_pairs={{0,32},{32,64},{64,96},{96,128},{128,160},{160,192},{192,224},{224... | collective-permute-start | bytes 626696 | tf_op jit(solution)/shard_map/ppermute | solution.py:42
  18.9 10.6 %collective-permute-start.2 = (bf16[48,2176]{1,0:T(8,128)(2,1)S(1)}, bf16[48,2176]{1,0:T(8,128)(2,1)S(1)}, u32[]{:S(2)}, u32[]{:S(2)}) collective-permute-start(bf16[48,2176]{1,0:T(8,128)(2,1)S(1)} %collective-permute-done.1.refs_2_), channel_id=1, source_target_pairs={{0,224},{32,0},{64,32},{96,64},{128,96},{160,128},{192,160},{224,1... | collective-permute-start | bytes 626696 | tf_op jit(solution)/shard_map/ppermute | solution.py:45
  25.2 7.9 %collective-permute-start.6 = (bf16[48,2176]{1,0:T(8,128)(2,1)S(1)}, bf16[48,2176]{1,0:T(8,128)(2,1)S(1)}, u32[]{:S(2)}, u32[]{:S(2)}) collective-permute-start(bf16[48,2176]{1,0:T(8,128)(2,1)S(1)} %collective-permute-done.5.refs_0_.refs_5_), channel_id=1, source_target_pairs={{0,32},{32,64},{64,96},{96,128},{128,160},{160,192},{192,224},{224... | collective-permute-start | bytes 626696 | tf_op jit(solution)/shard_map/ppermute | solution.py:42
  25.2 1.0 copy-start.6
  26.2 6.9 %collective-permute-start.7 = (bf16[48,2048]{1,0:T(8,128)(2,1)S(1)}, bf16[48,2048]{1,0:T(8,128)(2,1)S(1)}, u32[]{:S(2)}, u32[]{:S(2)}) collective-permute-start(bf16[48,2048]{1,0:T(8,128)(2,1)S(1)} %narrow.1.refs_0_), channel_id=1, source_target_pairs={{0,224},{32,0},{64,32},{96,64},{128,96},{160,128},{192,160},{224,1... | collective-permute-start | bytes 589832 | tf_op jit(solution)/shard_map/ppermute | solution.py:42
  33.1 0.9 copy-start.5
  36.5 34.0 %all-to-all-start = ((bf16[16,32,2048]{2,1,0:T(8,128)(2,1)}), bf16[16,32,2048]{2,1,0:T(8,128)(2,1)S(1)}, u32[]{:S(2)}, u32[]{:S(2)}) async-start(bf16[16,32,2048]{2,1,0:T(8,128)(2,1)} %bitcast.44), calls=%async_computation | async-start | bytes 4194304 | tf_op jit(solution)/shard_map/all_to_all | solution.py:349
  43.6 7.0 %collective-permute-start.11 = (bf16[48,2048]{1,0:T(8,128)(2,1)S(1)}, bf16[48,2048]{1,0:T(8,128)(2,1)S(1)}, u32[]{:S(2)}, u32[]{:S(2)}) collective-permute-start(bf16[48,2048]{1,0:T(8,128)(2,1)S(1)} %narrow.1.refs_0_), channel_id=1, source_target_pairs={{0,32},{32,64},{64,96},{96,128},{128,160},{160,192},{192,224},{224... | collective-permute-start | bytes 589832 | tf_op jit(solution)/shard_map/ppermute | solution.py:45
  47.4 7.3 %collective-permute-start.8 = (bf16[48,2048]{1,0:T(8,128)(2,1)S(1)}, bf16[48,2048]{1,0:T(8,128)(2,1)S(1)}, u32[]{:S(2)}, u32[]{:S(2)}) collective-permute-start(bf16[48,2048]{1,0:T(8,128)(2,1)S(1)} %collective-permute-done.7.refs_8_.refs_1_), channel_id=1, source_target_pairs={{0,224},{32,0},{64,32},{96,64},{128,96},{160,128},{192,160},{224,1... | collective-permute-start | bytes 589832 | tf_op jit(solution)/shard_map/ppermute | solution.py:42
  47.4 30.6 %collective-permute-start.15 = (bf16[2048,384]{1,0:T(8,128)(2,1)}, bf16[2048,384]{1,0:T(8,128)(2,1)}, u32[]{:S(2)}, u32[]{:S(2)}) collective-permute-start(bf16[2048,384]{1,0:T(8,128)(2,1)} %bitcast.45), channel_id=1, source_target_pairs={{0,1},{1,0},{2,3},{3,2},{4,5},{5,4},{6,7},{7,6},{8,9},{9,8},{10,11... | collective-permute-start | bytes 4718600 | tf_op jit(solution)/shard_map/ppermute | solution.py:366
  50.6 6.9 %collective-permute-start.12 = (bf16[48,2048]{1,0:T(8,128)(2,1)S(1)}, bf16[48,2048]{1,0:T(8,128)(2,1)S(1)}, u32[]{:S(2)}, u32[]{:S(2)}) collective-permute-start(bf16[48,2048]{1,0:T(8,128)(2,1)S(1)} %collective-permute-done.11.refs_7_), channel_id=1, source_target_pairs={{0,32},{32,64},{64,96},{96,128},{128,160},{160,192},{192,224},{224... | collective-permute-start | bytes 589832 | tf_op jit(solution)/shard_map/ppermute | solution.py:45
  54.7 6.4 %collective-permute-start.9 = (bf16[48,2048]{1,0:T(8,128)(2,1)S(1)}, bf16[48,2048]{1,0:T(8,128)(2,1)S(1)}, u32[]{:S(2)}, u32[]{:S(2)}) collective-permute-start(bf16[48,2048]{1,0:T(8,128)(2,1)S(1)} %collective-permute-done.8.refs_2_), channel_id=1, source_target_pairs={{0,224},{32,0},{64,32},{96,64},{128,96},{160,128},{192,160},{224,1... | collective-permute-start | bytes 589832 | tf_op jit(solution)/shard_map/ppermute | solution.py:42
  54.7 25.5 %collective-permute-start.16 = (bf16[2048,384]{1,0:T(8,128)(2,1)}, bf16[2048,384]{1,0:T(8,128)(2,1)}, u32[]{:S(2)}, u32[]{:S(2)}) collective-permute-start(bf16[2048,384]{1,0:T(8,128)(2,1)} %bitcast.47), channel_id=1, source_target_pairs={{0,1},{1,0},{2,3},{3,2},{4,5},{5,4},{6,7},{7,6},{8,9},{9,8},{10,11... | collective-permute-start | bytes 4718600 | tf_op jit(solution)/shard_map/ppermute | solution.py:366
  57.5 6.9 %collective-permute-start.13 = (bf16[48,2048]{1,0:T(8,128)(2,1)S(1)}, bf16[48,2048]{1,0:T(8,128)(2,1)S(1)}, u32[]{:S(2)}, u32[]{:S(2)}) collective-permute-start(bf16[48,2048]{1,0:T(8,128)(2,1)S(1)} %collective-permute-done.12.refs_6_), channel_id=1, source_target_pairs={{0,32},{32,64},{64,96},{96,128},{128,160},{160,192},{192,224},{224... | collective-permute-start | bytes 589832 | tf_op jit(solution)/shard_map/ppermute | solution.py:45
  61.1 6.0 %collective-permute-start.10 = (bf16[48,2048]{1,0:T(8,128)(2,1)S(1)}, bf16[48,2048]{1,0:T(8,128)(2,1)S(1)}, u32[]{:S(2)}, u32[]{:S(2)}) collective-permute-start(bf16[48,2048]{1,0:T(8,128)(2,1)S(1)} %collective-permute-done.9.refs_3_), channel_id=1, source_target_pairs={{0,224},{32,0},{64,32},{96,64},{128,96},{160,128},{192,160},{224,1... | collective-permute-start | bytes 589832 | tf_op jit(solution)/shard_map/ppermute | solution.py:42
  70.6 1.4 copy-start.2
  72.0 32.7 %all-to-all-start.1 = ((bf16[16,32,2048]{2,1,0:T(8,128)(2,1)}), bf16[16,32,2048]{2,1,0:T(8,128)(2,1)}, u32[]{:S(2)}, u32[]{:S(2)}) async-start(bf16[16,32,2048]{2,1,0:T(8,128)(2,1)} %bitcast.43), calls=%async_computation.1 | async-start | bytes 4194304 | tf_op jit(solution)/shard_map/all_to_all | solution.py:349
  77.9 2.4 %copy-start.7 = (bf16[1,2048,384]{2,1,0:T(8,128)(2,1)S(1)}, bf16[1,2048,384]{2,1,0:T(8,128)(2,1)}, u32[]{:S(2)}) copy-start(bf16[1,2048,384]{2,1,0:T(8,128)(2,1)} %param.12) | copy-start | bytes 4718596
  77.9 5.2 %collective-permute-start.14 = (bf16[2048,384]{1,0:T(8,128)(2,1)}, bf16[2048,384]{1,0:T(8,128)(2,1)S(1)}, u32[]{:S(2)}, u32[]{:S(2)}) collective-permute-start(bf16[2048,384]{1,0:T(8,128)(2,1)} %bitcast.49), channel_id=1, source_target_pairs={{0,1},{1,0},{2,3},{3,2},{4,5},{5,4},{6,7},{7,6},{8,9},{9,8},{10,11... | collective-permute-start | bytes 4718600 | tf_op jit(solution)/shard_map/ppermute | solution.py:366
  80.2 5.0 %copy-start = (bf16[2048,768]{1,0:T(8,128)(2,1)}, bf16[2048,768]{1,0:T(8,128)(2,1)S(1)}, u32[]{:S(2)}) copy-start(bf16[2048,768]{1,0:T(8,128)(2,1)S(1)} %pad_maximum_fusion.1.wg_ref.wg_h) | copy-start | bytes 9437188
  80.2 3.0 %copy-start.8 = (bf16[1,2048,384]{2,1,0:T(8,128)(2,1)S(1)}, bf16[1,2048,384]{2,1,0:T(8,128)(2,1)}, u32[]{:S(2)}) copy-start(bf16[1,2048,384]{2,1,0:T(8,128)(2,1)} %param.13) | copy-start | bytes 4718596
  83.1 2.9 %copy-start.1 = (bf16[2048,768]{1,0:T(8,128)(2,1)}, bf16[2048,768]{1,0:T(8,128)(2,1)S(1)}, u32[]{:S(2)}) copy-start(bf16[2048,768]{1,0:T(8,128)(2,1)S(1)} %pad_maximum_fusion.2.wu_ref.wu_h) | copy-start | bytes 9437188
  83.1 3.2 %copy-start.3 = (bf16[16,32,2048]{2,1,0:T(8,128)(2,1)S(1)}, bf16[16,32,2048]{2,1,0:T(8,128)(2,1)}, u32[]{:S(2)}) copy-start(bf16[16,32,2048]{2,1,0:T(8,128)(2,1)} %copy-done.2) | copy-start | bytes 6291460
  116.0 8.5 %copy-start.11 = (bf16[512,768]{1,0:T(8,128)(2,1)S(1)}, bf16[512,768]{1,0:T(8,128)(2,1)}, u32[]{:S(2)}) copy-start(bf16[512,768]{1,0:T(8,128)(2,1)} %get-tuple-element.23) | copy-start | bytes 2359300
  116.0 58.5 %all-to-all-start.2 = ((bf16[128,4,2048]{2,1,0:T(4,128)(2,1)}), bf16[128,4,2048]{2,1,0:T(4,128)(2,1)S(1)}, u32[]{:S(2)}, u32[]{:S(2)}) async-start(bf16[128,4,2048]{2,1,0:T(4,128)(2,1)} %get-tuple-element.20), calls=%async_computation.2 | async-start | bytes 4194304 | tf_op jit(solution)/shard_map/all_to_all | solution.py:372
  124.5 3.2 %copy-start.4 = (bf16[16,32,2048]{2,1,0:T(8,128)(2,1)S(1)}, bf16[16,32,2048]{2,1,0:T(8,128)(2,1)}, u32[]{:S(2)}) copy-start(bf16[16,32,2048]{2,1,0:T(8,128)(2,1)} %copy-done.2) | copy-start | bytes 6291460
  124.5 3.2 %copy-start.12 = (bf16[512,768]{1,0:T(8,128)(2,1)S(1)}, bf16[512,768]{1,0:T(8,128)(2,1)}, u32[]{:S(2)}) copy-start(bf16[512,768]{1,0:T(8,128)(2,1)} %get-tuple-element.22) | copy-start | bytes 2359300
  127.5 3.9 %collective-permute-start.19 = (bf16[2048,384]{1,0:T(8,128)(2,1)S(1)}, bf16[2048,384]{1,0:T(8,128)(2,1)S(1)}, u32[]{:S(2)}, u32[]{:S(2)}) collective-permute-start(bf16[2048,384]{1,0:T(8,128)(2,1)S(1)} %convolution_convert_fusion), channel_id=1, source_target_pairs={{0,1},{1,0},{2,3},{3,2},{4,5},{5,4},{6,7},{7,6},{8,9},{9,8},{10,11... | collective-permute-start | bytes 4718600 | tf_op jit(solution)/shard_map/ppermute | solution.py:377
  127.7 1.9 %copy-start.10 = (bf16[512,768]{1,0:T(8,128)(2,1)S(1)}, bf16[512,768]{1,0:T(8,128)(2,1)}, u32[]{:S(2)}) copy-start(bf16[512,768]{1,0:T(8,128)(2,1)} %get-tuple-element.21) | copy-start | bytes 2359300
  129.0 6.5 %collective-permute-start.18 = (bf16[2048,384]{1,0:T(8,128)(2,1)S(1)}, bf16[2048,384]{1,0:T(8,128)(2,1)S(1)}, u32[]{:S(2)}, u32[]{:S(2)}) collective-permute-start(bf16[2048,384]{1,0:T(8,128)(2,1)S(1)} %convolution_convert_fusion.2), channel_id=1, source_target_pairs={{0,1},{1,0},{2,3},{3,2},{4,5},{5,4},{6,7},{7,6},{8,9},{9,8},{10,11... | collective-permute-start | bytes 4718600 | tf_op jit(solution)/shard_map/ppermute | solution.py:377
  129.5 1.5 copy-start.9
  130.8 7.2 %collective-permute-start.17 = (bf16[2048,384]{1,0:T(8,128)(2,1)S(1)}, bf16[2048,384]{1,0:T(8,128)(2,1)S(1)}, u32[]{:S(2)}, u32[]{:S(2)}) collective-permute-start(bf16[2048,384]{1,0:T(8,128)(2,1)S(1)} %convolution_convert_fusion.4), channel_id=1, source_target_pairs={{0,1},{1,0},{2,3},{3,2},{4,5},{5,4},{6,7},{7,6},{8,9},{9,8},{10,11... | collective-permute-start | bytes 4718600 | tf_op jit(solution)/shard_map/ppermute | solution.py:377
